TPU v7x, 32 devices: a whole 2x2x4 slice. The times are simulated.
32 devices in a mesh: dp: 8 (over z, y), tensor: 4 (over x, core).
Axes of the slice: x: 2, y: 2, z: 4, core: 2. Of those that a mesh axis runs over, the one named last changes fastest.
Arguments:
- layer_input_rows: bfloat16 [32768, 768], P(('dp', 'tensor')), may hold values from -6 to 6
- output_gradient: bfloat16 [32768, 768], P(('dp', 'tensor')), may hold values from -6 to 6
- query_weight: bfloat16 [768, 768], P('dp', 'tensor'), may hold values from -0.21875 to 0.21875
- key_weight: bfloat16 [768, 768], P('dp', 'tensor'), may hold values from -0.21875 to 0.21875
- value_weight: bfloat16 [768, 768], P('dp', 'tensor'), may hold values from -0.21875 to 0.21875
- output_weight: bfloat16 [768, 768], P('tensor', 'dp'), may hold values from -1.75 to 1.75
- up_weight: bfloat16 [768, 3072], P('dp', 'tensor'), may hold values from -0.21875 to 0.21875
- down_weight: bfloat16 [3072, 768], P('tensor', 'dp'), may hold values from -0.109375 to 0.109375
- query_bias_vector: float32 [768], P('tensor'), may hold values from -3 to 3
- value_bias_vector: float32 [768], P('tensor'), may hold values from -3 to 3
- output_bias_vector: float32 [768], replicated, may hold values from -5 to 5
- up_bias_vector: float32 [3072], P('tensor'), may hold values from -3 to 3
- down_bias_vector: float32 [768], replicated, may hold values from -2 to 2
- query_down_frozen: bfloat16 [768, 8], replicated, may hold values from -0.21875 to 0.21875
- value_down_frozen: bfloat16 [768, 8], replicated, may hold values from -0.21875 to 0.21875
- query_up_trained: bfloat16 [8, 768], P(None, 'tensor'), may hold values from -0.59765625 to 0.59765625
- value_up_trained: bfloat16 [8, 768], P(None, 'tensor'), may hold values from -0.59765625 to 0.59765625
- first_norm_gain: float32 [768], replicated, may hold values from 0.5 to 1.5
- first_norm_bias: float32 [768], replicated, may hold values from -2 to 2
- second_norm_gain: float32 [768], replicated, may hold values from 0.5 to 1.5
- second_norm_bias: float32 [768], replicated, may hold values from -2 to 2
- segments: int32 [32768], P('dp'), may hold values from 0 to 48, as said below
- sentence_row_mask: int32 [32768], P('dp'), may hold values from 0 to 1, as said below
Outputs:
- output: bfloat16 [32768, 768], P(('dp', 'tensor'))
- grad_input: bfloat16 [32768, 768], P(('dp', 'tensor'))
- grad_lora_query: float32 [8, 768], P(None, 'tensor')
- grad_lora_value: float32 [8, 768], P(None, 'tensor')
Inputs may be any that keep to these rules, and one draw needn't show every extreme that they name: `segments`: ids restart at 0 in every sequence of 512 rows and rise by one at each sentence boundary; sentences hold 8 to 128 rows, and the first sentence of every sequence holds exactly 128 rows; in the first sequence of all rows every later sentence holds exactly 8 rows; the padding rows at a sequence's end share one more id. `sentence_row_mask`: in each sequence of 512 rows the rows after the last sentence that ends before row 512 are 0, from 1 to 128 of them; all others are 1.
All inputs are finite; a program needn't handle non-finite values.
Results may differ from a plain program's by a relative error of at most 0.02.
Values may be sent and summed in bfloat16 or wider, within the bound.
A program may use at most 128 MiB of HBM per device.

v0:
```python
import jax
import jax.numpy as jnp
from jax import lax
from jax.sharding import PartitionSpec as P

HEAD_DIM = 64
ADAPTER_RANK = 8
ADAPTER_NUMER = 16
SEQ = 512


TOP_PRECISION = lax.Precision.HIGHEST
EPSILON = 1e-05
NEG_FILL = -1e30


def layer_norm(row_matrix, gain, shift):
    mean = jnp.mean(row_matrix, axis=-1, keepdims=True)
    centered = row_matrix - mean
    variance = jnp.mean(centered * centered, axis=-1, keepdims=True)
    inverse = lax.rsqrt(variance + EPSILON)
    normed = centered * inverse
    return (normed * gain + shift, normed, inverse)


def norm_back(grad, normed, inverse, gain):
    scaled = grad * gain
    centered = scaled - jnp.mean(scaled, axis=-1, keepdims=True)
    return inverse * (centered - normed * jnp.mean(scaled * normed, axis=-1, keepdims=True))


def allowed_keys(segment_ids, live_flags):
    places = jnp.arange(segment_ids.shape[0])
    same = (segment_ids[:, None] == segment_ids[None, :]) & (live_flags[None, :] == 1)
    return same | (places[:, None] == places[None, :])


def masked_scores(query_rows, keys, segment_ids, live_flags):
    scale = HEAD_DIM ** (-0.5)
    scores = (
        jnp.einsum("qhd,khd->hqk", query_rows, keys, preferred_element_type=jnp.float32) * scale
    )
    return jnp.where(allowed_keys(segment_ids, live_flags)[None], scores, NEG_FILL)


def attend(inputs):
    query_rows, keys, value_rows, segment_ids, live_flags = inputs
    scores = masked_scores(query_rows, keys, segment_ids, live_flags)
    highest = jnp.max(scores, axis=-1, keepdims=True)
    powers = jnp.exp(scores - highest)
    total_sum = jnp.sum(powers, axis=-1, keepdims=True)
    weights = (powers / total_sum).astype(jnp.bfloat16)
    context = jnp.einsum("hqk,khd->qhd", weights, value_rows, preferred_element_type=jnp.float32)
    return (context.astype(jnp.bfloat16), (highest + jnp.log(total_sum))[..., 0])


def attend_back(inputs):
    query_rows, keys, value_rows, grad_context, log_total, segment_ids, live_flags = inputs
    scale = HEAD_DIM ** (-0.5)
    scores = masked_scores(query_rows, keys, segment_ids, live_flags)
    probs = jnp.exp(scores - log_total[..., None])
    grad_probs = jnp.einsum(
        "qhd,khd->hqk", grad_context, value_rows, preferred_element_type=jnp.float32
    )
    inner = jnp.sum(probs * grad_probs, axis=-1, keepdims=True)
    grad_scores = (probs * (grad_probs - inner)).astype(jnp.bfloat16)
    query_gradient_rows = (
        jnp.einsum("hqk,khd->qhd", grad_scores, keys, preferred_element_type=jnp.float32) * scale
    ).astype(jnp.bfloat16)
    grad_keys = (
        jnp.einsum("hqk,qhd->khd", grad_scores, query_rows, preferred_element_type=jnp.float32)
        * scale
    ).astype(jnp.bfloat16)
    value_gradient_rows = jnp.einsum(
        "hqk,qhd->khd", probs.astype(jnp.bfloat16), grad_context, preferred_element_type=jnp.float32
    ).astype(jnp.bfloat16)
    return (query_gradient_rows, grad_keys, value_gradient_rows)


def body(
    layer_input_rows,
    output_gradient,
    query_weight,
    key_weight,
    value_weight,
    output_weight,
    up_weight,
    down_weight,
    query_bias_vector,
    value_bias_vector,
    output_bias_vector,
    up_bias_vector,
    down_bias_vector,
    query_down_frozen,
    value_down_frozen,
    query_up_trained,
    value_up_trained,
    first_norm_gain,
    first_norm_bias,
    second_norm_gain,
    second_norm_bias,
    segments,
    sentence_row_mask,
):
    wide_matrix = jnp.float32
    narrow_matrix = jnp.bfloat16
    adapter_scale = ADAPTER_NUMER / ADAPTER_RANK
    full_query, full_key, full_value, full_out, full_up, full_down = (
        lax.all_gather(query_weight, "dp", axis=0, tiled=True),
        lax.all_gather(key_weight, "dp", axis=0, tiled=True),
        lax.all_gather(value_weight, "dp", axis=0, tiled=True),
        lax.all_gather(output_weight, "dp", axis=1, tiled=True),
        lax.all_gather(up_weight, "dp", axis=0, tiled=True),
        lax.all_gather(down_weight, "dp", axis=1, tiled=True),
    )
    width_size = full_query.shape[1]
    adapter_down_pass = jnp.concatenate([query_down_frozen, value_down_frozen], axis=1)
    piece_rows = lax.all_gather(layer_input_rows, "tensor", axis=0, tiled=True)
    adapter_input = jnp.dot(
        piece_rows, adapter_down_pass, preferred_element_type=wide_matrix
    ).astype(narrow_matrix)
    query_before_heads = (
        jnp.dot(piece_rows, full_query, preferred_element_type=wide_matrix)
        + query_bias_vector
        + adapter_scale
        * jnp.dot(
            adapter_input[:, :ADAPTER_RANK], query_up_trained, preferred_element_type=wide_matrix
        )
    )
    key_before_heads = jnp.dot(piece_rows, full_key, preferred_element_type=wide_matrix)
    value_before_heads = (
        jnp.dot(piece_rows, full_value, preferred_element_type=wide_matrix)
        + value_bias_vector
        + adapter_scale
        * jnp.dot(
            adapter_input[:, ADAPTER_RANK:], value_up_trained, preferred_element_type=wide_matrix
        )
    )
    projected_rows = jnp.concatenate(
        [
            query_before_heads.astype(narrow_matrix),
            key_before_heads.astype(narrow_matrix),
            value_before_heads.astype(narrow_matrix),
            adapter_input,
        ],
        axis=1,
    )
    rows_all = projected_rows.shape[0]
    seq_count = rows_all // SEQ
    heads_here = width_size // HEAD_DIM

    def by_heads(block):
        return block.reshape(seq_count, SEQ, heads_here, HEAD_DIM)

    query_rows = by_heads(projected_rows[:, :width_size])
    keys = by_heads(projected_rows[:, width_size : 2 * width_size])
    value_rows = by_heads(projected_rows[:, 2 * width_size : 3 * width_size])
    adapter_row_output = projected_rows[:, 3 * width_size :]
    segment_blocks = segments.reshape(seq_count, SEQ)
    live_blocks = sentence_row_mask.reshape(seq_count, SEQ)
    context, log_total = lax.map(
        attend, (query_rows, keys, value_rows, segment_blocks, live_blocks)
    )
    context = context.reshape(rows_all, width_size)
    attn_part = lax.psum_scatter(
        jnp.dot(context, full_out, preferred_element_type=wide_matrix).astype(jnp.bfloat16),
        "tensor",
        scatter_dimension=0,
        tiled=True,
    ).astype(jnp.float32)
    first_out, first_normed, first_inverse = layer_norm(
        layer_input_rows.astype(wide_matrix) + attn_part + output_bias_vector,
        first_norm_gain,
        first_norm_bias,
    )
    middle = first_out.astype(narrow_matrix)
    inner = (
        jnp.dot(
            lax.all_gather(middle, "tensor", axis=0, tiled=True),
            full_up,
            preferred_element_type=wide_matrix,
        )
        + up_bias_vector
    )
    active = jax.nn.gelu(inner, approximate=False).astype(narrow_matrix)
    ffn_part = lax.psum_scatter(
        jnp.dot(active, full_down, preferred_element_type=wide_matrix).astype(jnp.bfloat16),
        "tensor",
        scatter_dimension=0,
        tiled=True,
    ).astype(jnp.float32)
    output, second_normed, second_inverse = layer_norm(
        first_out + ffn_part + down_bias_vector, second_norm_gain, second_norm_bias
    )
    grad_second = norm_back(
        output_gradient.astype(wide_matrix), second_normed, second_inverse, second_norm_gain
    )
    grad_branch = grad_second.astype(narrow_matrix)
    grad_gathered = lax.all_gather(grad_branch, "tensor", axis=0, tiled=True)

    def inner_back(piece_rows):
        grad_active = jnp.einsum(
            "rd,fd->rf", grad_gathered, full_down, preferred_element_type=wide_matrix
        )
        inner = jnp.dot(piece_rows, full_up, preferred_element_type=wide_matrix) + up_bias_vector
        slope = jax.vjp(lambda value: jax.nn.gelu(value, approximate=False), inner)[1]
        return slope(grad_active)[0].astype(narrow_matrix)

    grad_inner = inner_back(lax.all_gather(middle, "tensor", axis=0, tiled=True))
    grad_middle = lax.psum_scatter(
        jnp.einsum("rf,df->rd", grad_inner, full_up, preferred_element_type=wide_matrix).astype(
            jnp.bfloat16
        ),
        "tensor",
        scatter_dimension=0,
        tiled=True,
    ).astype(jnp.float32)
    grad_first = norm_back(grad_second + grad_middle, first_normed, first_inverse, first_norm_gain)
    grad_attn = grad_first.astype(narrow_matrix)
    grad_context = jnp.einsum(
        "rd,wd->rw",
        lax.all_gather(grad_attn, "tensor", axis=0, tiled=True),
        full_out,
        preferred_element_type=wide_matrix,
    ).astype(narrow_matrix)
    query_gradient_rows, grad_keys, value_gradient_rows = lax.map(
        attend_back,
        (
            query_rows,
            keys,
            value_rows,
            by_heads(grad_context),
            log_total,
            segment_blocks,
            live_blocks,
        ),
    )
    query_gradient_rows = query_gradient_rows.reshape(rows_all, width_size)
    grad_keys = grad_keys.reshape(rows_all, width_size)
    value_gradient_rows = value_gradient_rows.reshape(rows_all, width_size)
    adapter_backward = (
        jnp.concatenate(
            [
                jnp.einsum(
                    "zs,os->zo",
                    query_gradient_rows,
                    query_up_trained,
                    preferred_element_type=wide_matrix,
                ),
                jnp.einsum(
                    "zs,os->zo",
                    value_gradient_rows,
                    value_up_trained,
                    preferred_element_type=wide_matrix,
                ),
            ],
            axis=1,
        )
        * adapter_scale
    )
    adapter_down_broad = adapter_down_pass.astype(wide_matrix)
    total_sum = jnp.einsum(
        "rw,dw->rd", query_gradient_rows, full_query, preferred_element_type=wide_matrix
    )
    total_sum = total_sum + jnp.einsum(
        "rw,dw->rd", grad_keys, full_key, preferred_element_type=wide_matrix
    )
    total_sum = total_sum + jnp.einsum(
        "rw,dw->rd", value_gradient_rows, full_value, preferred_element_type=wide_matrix
    )
    grad_rows = lax.psum_scatter(
        (
            total_sum
            + jnp.einsum("se,pe->sp", adapter_backward, adapter_down_broad, precision=TOP_PRECISION)
        ).astype(jnp.bfloat16),
        "tensor",
        scatter_dimension=0,
        tiled=True,
    ).astype(jnp.float32)
    grad_input = (grad_first + grad_rows).astype(narrow_matrix)
    grad_lq = (
        jnp.einsum(
            "yh,yj->hj",
            adapter_row_output[:, :ADAPTER_RANK],
            query_gradient_rows,
            preferred_element_type=wide_matrix,
        )
        * adapter_scale
    )
    grad_lv = (
        jnp.einsum(
            "yh,yj->hj",
            adapter_row_output[:, ADAPTER_RANK:],
            value_gradient_rows,
            preferred_element_type=wide_matrix,
        )
        * adapter_scale
    )
    grad_lq, grad_lv = lax.psum((grad_lq, grad_lv), "dp")
    return (output.astype(narrow_matrix), grad_input, grad_lq, grad_lv)


def solution(mesh):
    in_specs = (
        P(("dp", "tensor"), None),
        P(("dp", "tensor"), None),
        P("dp", "tensor"),
        P("dp", "tensor"),
        P("dp", "tensor"),
        P("tensor", "dp"),
        P("dp", "tensor"),
        P("tensor", "dp"),
        P("tensor"),
        P("tensor"),
        P(),
        P("tensor"),
        P(),
        P(),
        P(),
        P(None, "tensor"),
        P(None, "tensor"),
        P(),
        P(),
        P(),
        P(),
        P("dp"),
        P("dp"),
    )
    out_specs = (
        P(("dp", "tensor"), None),
        P(("dp", "tensor"), None),
        P(None, "tensor"),
        P(None, "tensor"),
    )
    return jax.shard_map(body, mesh=mesh, in_specs=in_specs, out_specs=out_specs, check_vma=False)
```

profile of v0, /device:TPU:0, one launch (start us, length us, event | category | flops | bytes accessed | tf_op | source)
XLA Modules:
  0.0 848.9 jit_solution(7653134638666144229)
XLA Ops:
  13.8 33.1 %all_gather.32 = bf16[768,192]{1,0:T(8,128)(2,1)S(1)} all-gather(bf16[96,192]{1,0:T(8,128)(2,1)} %param.31), channel_id=1, replica_groups=mesh['dp'=8,'tensor'=4] {'dp'}, dimensions={0}, use_global_device_ids=true | all-gather | bytes 331776 | tf_op jit(solution)/shard_map/all_gather | solution.py:111
  46.9 31.5 %all_gather.33 = bf16[768,192]{1,0:T(8,128)(2,1)S(1)} all-gather(bf16[96,192]{1,0:T(8,128)(2,1)} %param.29), channel_id=1, replica_groups=mesh['dp'=8,'tensor'=4] {'dp'}, dimensions={0}, use_global_device_ids=true | all-gather | bytes 331776 | tf_op jit(solution)/shard_map/all_gather | solution.py:109
  78.4 31.3 %all_gather.34 = bf16[768,192]{1,0:T(8,128)(2,1)S(1)} all-gather(bf16[96,192]{1,0:T(8,128)(2,1)} %param.30), channel_id=1, replica_groups=mesh['dp'=8,'tensor'=4] {'dp'}, dimensions={0}, use_global_device_ids=true | all-gather | bytes 331776 | tf_op jit(solution)/shard_map/all_gather | solution.py:110
  109.7 31.0 %all_gather.35 = bf16[192,768]{0,1:T(8,128)(2,1)S(1)} all-gather(bf16[192,96]{0,1:T(8,128)(2,1)S(1)} %copy.61), channel_id=1, replica_groups=mesh['dp'=8,'tensor'=4] {'dp'}, dimensions={1}, use_global_device_ids=true | all-gather | bytes 331776 | tf_op jit(solution)/shard_map/all_gather | solution.py:112
  140.7 4.7 fusion.68
  145.4 2.2 convolution_add_fusion.1
  149.0 1.6 copy.57
  150.6 2.2 convolution_add_fusion
  154.6 2.2 convolution_convert_fusion.4
  159.4 52.3 %while.26 = (s32[]{:T(128)}, bf16[8,512,3,64]{1,3,2,0:T(8,128)(2,1)}, f32[8,3,512]{2,1,0:T(4,128)}, bf16[8,512,3,64]{1,3,2,0:T(8,128)(2,1)}, s32[8,512]{1,0:T(8,...) while((s32[]{:T(128)}, ...), condition=%wide.region_3.4_spmd, body=%wide.region_0.3_spmd.sunk | while | flops 211909632 | bytes 11334769 | solution.py:161
  162.8 2.7 fusion.153
  169.3 2.7 fusion.153
  175.8 2.7 fusion.153
  182.3 2.7 fusion.153
  188.8 2.7 fusion.153
  195.3 2.7 fusion.153
  201.9 2.7 fusion.153
  208.4 2.7 fusion.153
  211.7 3.4 copy.60
  215.8 4.6 convolution_convert_fusion
  221.0 58.8 %reduce-scatter.5.cloned.1.call-done = bf16[1024,768]{1,0:T(8,128)(2,1)} async-done(((bf16[4096,768]{1,0:T(8,128)(2,1)}), bf16[1024,768]{1,0:T(8,128)(2,1)}) %reduce-scatter.5.cloned.1.call-update) | async-done | bytes 1572880 | tf_op jit(solution)/shard_map/reduce_scatter | solution.py:165
  279.8 2.1 fusion.71
  282.9 2.0 fusion.70
  285.6 45.7 %all-gather.9.cloned.1.call-done = bf16[4096,768]{1,0:T(8,128)(2,1)} async-done(((bf16[1024,768]{1,0:T(8,128)(2,1)}), bf16[4096,768]{1,0:T(8,128)(2,1)}) %all-gather.9.cloned.1.call-update) | async-done | bytes 6291472 | tf_op jit(solution)/shard_map/all_gather | solution.py:179
  331.3 34.0 %fusion.56 = (f32[4096,768]{1,0:T(8,128)}, f32[4096,768]{1,0:T(8,128)}) fusion(f32[768]{0:T(1024)S(1)} %copy-done.34, bf16[4096,768]{1,0:T(8,128)(2,1)} %all-gather.9.cloned.1.call-done, bf16[768,768]{1,0:T(8,128)(2,1)} %all-gather.11.cloned.1.call-done), kind=kOutput, calls=%fused_computation.68 | convolution fusion | flops 5030019072 | bytes 32640000 | tf_op jit(solution)/shard_map/dot_general | solution.py:178
  365.3 9.8 %all-gather.13.cloned.1.call-done = bf16[768,768]{0,1:T(8,128)(2,1)} async-done(((bf16[768,96]{0,1:T(8,128)(2,1)}), bf16[768,768]{0,1:T(8,128)(2,1)}) %all-gather.13.cloned.1.call-update) | async-done | bytes 1179664 | tf_op jit(solution)/shard_map/all_gather | solution.py:114
  375.2 12.9 %convolution_convert_fusion.2 = bf16[4096,768]{1,0:T(8,128)(2,1)} fusion(bf16[768,768]{0,1:T(8,128)(2,1)} %all-gather.13.cloned.1.call-done, f32[4096,768]{1,0:T(8,128)} %get-tuple-element.223, f32[4096,768]{1,0:T(8,128)} %get-tuple-element.224, f32[768]{0:T(1024)S(1)} %copy-done.34), kind=kOutput, calls=%fused_computation.87 | convolution fusion | flops 4847566848 | bytes 32640000 | tf_op jit(solution)/shard_map/dot_general | solution.py:187
  388.1 56.7 %reduce-scatter.7.cloned.1.call-done = bf16[1024,768]{1,0:T(8,128)(2,1)} async-done(((bf16[4096,768]{1,0:T(8,128)(2,1)}), bf16[1024,768]{1,0:T(8,128)(2,1)}) %reduce-scatter.7.cloned.1.call-update) | async-done | bytes 1572880 | tf_op jit(solution)/shard_map/reduce_scatter | solution.py:186
  444.9 2.9 fusion.89
  450.3 3.4 fusion.88
  453.8 46.5 %all-gather.15.cloned.1.call-done = bf16[4096,768]{1,0:T(8,128)(2,1)} async-done(((bf16[1024,768]{1,0:T(8,128)(2,1)}), bf16[4096,768]{1,0:T(8,128)(2,1)}) %all-gather.15.cloned.1.call-update) | async-done | bytes 6291472 | tf_op jit(solution)/shard_map/all_gather | solution.py:199
  500.3 20.2 %convolution_convert_fusion.1 = bf16[4096,768]{1,0:T(8,128)(2,1)} fusion(bf16[768,768]{1,0:T(8,128)(2,1)} %all-gather.11.cloned.1.call-done, f32[4096,768]{1,0:T(8,128)} %get-tuple-element.223, f32[4096,768]{1,0:T(8,128)} %get-tuple-element.224, f32[768]{0:T(1024)S(1)} %copy-done.34, bf16[4096,768]{1,0:T(8,128)(2,1)} %all-gather.15.cloned.1.call-done, ...), kind=kOutput, calls=%fused_computation.86 | convolution fusion | flops 9714008064 | bytes 40111104 | tf_op jit(solution)/shard_map/rf,df->rd/dot_general | solution.py:211
  520.5 58.3 %reduce-scatter.9.cloned.1.call-done = bf16[1024,768]{1,0:T(8,128)(2,1)} async-done(((bf16[4096,768]{1,0:T(8,128)(2,1)}), bf16[1024,768]{1,0:T(8,128)(2,1)}) %reduce-scatter.9.cloned.1.call-update) | async-done | bytes 1572880 | tf_op jit(solution)/shard_map/reduce_scatter | solution.py:210
  578.9 3.6 fusion.72
  582.6 3.0 fusion.87
  585.7 46.5 %all-gather.17.cloned.1.call-done = bf16[4096,768]{1,0:T(8,128)(2,1)} async-done(((bf16[1024,768]{1,0:T(8,128)(2,1)}), bf16[4096,768]{1,0:T(8,128)(2,1)}) %all-gather.17.cloned.1.call-update) | async-done | bytes 6291472 | tf_op jit(solution)/shard_map/all_gather | solution.py:222
  632.2 5.0 convolution_convert_fusion.3
  641.1 95.5 %while.27 = (s32[]{:T(128)}, bf16[8,512,3,64]{1,3,2,0:T(8,128)(2,1)S(1)}, bf16[8,512,3,64]{1,3,2,0:T(8,128)(2,1)}, bf16[8,512,3,64]{1,3,2,0:T(8,128)(2,1)}, bf16...) while((s32[]{:T(128)}, ...), condition=%wide.region_17.18_spmd, body=%wide.region_15.17_spmd.sunk | while | flops 511933440 | bytes 26128520 | solution.py:226
  641.1 1.5 fusion.162
  645.1 2.2 multiply_reduce_fusion.6
  649.6 2.2 fusion.165
  657.0 2.2 multiply_reduce_fusion.6
  661.5 2.2 fusion.165
  668.9 2.2 multiply_reduce_fusion.6
  673.4 2.2 fusion.165
  680.9 2.2 multiply_reduce_fusion.6
  685.3 2.2 fusion.165
  692.8 2.2 multiply_reduce_fusion.6
  697.2 2.2 fusion.165
  700.7 1.5 fusion.162
  704.7 2.2 multiply_reduce_fusion.6
  709.1 2.2 fusion.165
  716.6 2.2 multiply_reduce_fusion.6
  721.0 2.2 fusion.165
  724.5 1.5 fusion.162
  728.5 2.2 multiply_reduce_fusion.6
  732.9 2.2 fusion.165
  738.5 6.4 fusion.92
  748.7 6.4 fusion.93
  755.1 8.0 fusion.73
  763.1 16.0 %add_convert_fusion = bf16[4096,768]{1,0:T(8,128)(2,1)} fusion(f32[4096,768]{1,0:T(8,128)} %fusion.73, f32[4096,768]{1,0:T(8,128)} %fusion.92, f32[4096,768]{1,0:T(8,128)} %fusion.93, bf16[4096,192]{0,1:T(8,128)(2,1)S(1)} %bitcast.186, bf16[768,192]{1,0:T(8,128)(2,1)S(1)} %copy-done.12), kind=kOutput, calls=%fused_computation.69 | convolution fusion | flops 1220542464 | bytes 45907968 | tf_op jit(solution)/shard_map/rw,dw->rd/dot_general | solution.py:268
  781.0 37.7 %all-reduce = (f32[8,192]{1,0:T(8,128)}, f32[8,192]{1,0:T(8,128)}) all-reduce(f32[8,192]{1,0:T(8,128)S(1)} %convolution_multiply_fusion.5, f32[8,192]{1,0:T(8,128)S(1)} %convolution_multiply_fusion.4), channel_id=1, replica_groups=mesh['dp'=8,'tensor'=4] {'dp'}, use_global_device_ids=true, to_apply=%region_19.20 | all-reduce | flops 3072 | bytes 24576 | tf_op jit(solution)/shard_map/psum | solution.py:299
  818.7 18.8 %reduce-scatter.11.cloned.1.call-done = bf16[1024,768]{1,0:T(8,128)(2,1)} async-done(((bf16[4096,768]{1,0:T(8,128)(2,1)}), bf16[1024,768]{1,0:T(8,128)(2,1)}) %reduce-scatter.11.cloned.1.call-update) | async-done | bytes 1572880 | tf_op jit(solution)/shard_map/reduce_scatter | solution.py:271
  837.5 3.8 add_convert_fusion.3
  (241 shorter events, 113.8 us)
Async XLA Ops:
  8.0 144.9 %copy-start = (bf16[8,192]{1,0:T(8,128)(2,1)S(1)}, bf16[8,192]{1,0:T(8,128)(2,1)}, u32[]{:S(2)}) copy-start(bf16[8,192]{1,0:T(8,128)(2,1)} %param.42) | copy-start | bytes 9220
  8.0 132.6 %all-gather.7.cloned.1.call-start = ((), (), s32[]{:S(2)}) async-start(), calls=%async_computation.4 | async-start | bytes 7864320 | tf_op jit(solution)/shard_map/all_gather | solution.py:118
  8.7 271.0 %reduce-scatter.5.cloned.1.call-start = ((), (), s32[]{:S(2)}) async-start(), calls=%async_computation.5 | async-start | bytes 7864320 | tf_op jit(solution)/shard_map/reduce_scatter | solution.py:165
  13.8 131.6 %copy-start.21 = (bf16[768,16]{0,1:T(8,128)(2,1)}, bf16[768,16]{0,1:T(8,128)(2,1)S(1)}, u32[]{:S(2)}) copy-start(bf16[768,16]{0,1:T(8,128)(2,1)S(1)} %constant_dynamic-update-slice_fusion) | copy-start | bytes 73732
  46.9 98.5 %copy-start.11 = (bf16[768,192]{1,0:T(8,128)(2,1)}, bf16[768,192]{1,0:T(8,128)(2,1)S(1)}, u32[]{:S(2)}) copy-start(bf16[768,192]{1,0:T(8,128)(2,1)S(1)} %all_gather.32) | copy-start | bytes 884740
  78.4 72.2 %copy-start.17 = (bf16[768,192]{1,0:T(8,128)(2,1)}, bf16[768,192]{1,0:T(8,128)(2,1)S(1)}, u32[]{:S(2)}) copy-start(bf16[768,192]{1,0:T(8,128)(2,1)S(1)} %all_gather.33) | copy-start | bytes 884740
  109.7 44.9 %copy-start.15 = (bf16[768,192]{1,0:T(8,128)(2,1)}, bf16[768,192]{1,0:T(8,128)(2,1)S(1)}, u32[]{:S(2)}) copy-start(bf16[768,192]{1,0:T(8,128)(2,1)S(1)} %all_gather.34) | copy-start | bytes 884740
  140.7 75.1 %copy-start.13 = (bf16[192,768]{0,1:T(8,128)(2,1)}, bf16[192,768]{0,1:T(8,128)(2,1)S(1)}, u32[]{:S(2)}) copy-start(bf16[192,768]{0,1:T(8,128)(2,1)S(1)} %all_gather.35) | copy-start | bytes 884740
  140.7 4.7 copy-start.32
  140.7 4.8 copy-start.1
  145.4 7.4 copy-start.19
  145.4 2.3 copy-start.28
  148.3 2.3 copy-start.33
  211.7 4.1 copy-start.5
  211.7 4.1 copy-start.6
  220.4 59.4 %copy-start.2 = (bf16[1024,768]{1,0:T(8,128)(2,1)S(1)}, bf16[1024,768]{1,0:T(8,128)(2,1)}, u32[]{:S(2)}) copy-start(bf16[1024,768]{1,0:T(8,128)(2,1)} %param.27) | copy-start | bytes 4718596
  220.4 59.4 %copy-start.23 = (f32[768]{0:T(1024)S(1)}, f32[768]{0:T(1024)}, u32[]{:S(2)}) copy-start(f32[768]{0:T(1024)} %param.37) | copy-start | bytes 9220
  220.4 65.2 %all-gather.11.cloned.1.call-start = ((), (), s32[]{:S(2)}) async-start(), calls=%async_computation.7 | async-start | bytes 1327104 | tf_op jit(solution)/shard_map/all_gather | solution.py:113
  221.0 61.9 %copy-start.24 = (f32[768]{0:T(1024)S(1)}, f32[768]{0:T(1024)}, u32[]{:S(2)}) copy-start(f32[768]{0:T(1024)} %param.44) | copy-start | bytes 9220
  221.0 61.9 %copy-start.26 = (f32[768]{0:T(1024)S(1)}, f32[768]{0:T(1024)}, u32[]{:S(2)}) copy-start(f32[768]{0:T(1024)} %param.45) | copy-start | bytes 9220
  221.0 110.3 %all-gather.9.cloned.1.call-start = ((), (), s32[]{:S(2)}) async-start(), calls=%async_computation.6 | async-start | bytes 7864320 | tf_op jit(solution)/shard_map/all_gather | solution.py:179
  279.8 2.2 copy-start.3
  282.9 48.4 %copy-start.34 = (f32[768]{0:T(1024)S(1)}, f32[768]{0:T(1024)}, u32[]{:S(2)}) copy-start(f32[768]{0:T(1024)} %param.38) | copy-start | bytes 9220
  284.9 90.2 %all-gather.13.cloned.1.call-start = ((), (), s32[]{:S(2)}) async-start(), calls=%async_computation.8 | async-start | bytes 1327104 | tf_op jit(solution)/shard_map/all_gather | solution.py:114
  285.5 159.3 %reduce-scatter.7.cloned.1.call-start = ((), (), s32[]{:S(2)}) async-start(), calls=%async_computation.9 | async-start | bytes 7864320 | tf_op jit(solution)/shard_map/reduce_scatter | solution.py:186
  388.0 56.8 %copy-start.30 = (f32[768]{0:T(1024)S(1)}, f32[768]{0:T(1024)}, u32[]{:S(2)}) copy-start(f32[768]{0:T(1024)} %param.39) | copy-start | bytes 9220
  388.1 112.2 %all-gather.15.cloned.1.call-start = ((), (), s32[]{:S(2)}) async-start(), calls=%async_computation.10 | async-start | bytes 7864320 | tf_op jit(solution)/shard_map/all_gather | solution.py:199
  447.8 1.4 copy-start.7
  447.8 1.4 copy-start.27
  448.4 2.0 copy-start.31
  453.8 125.1 %reduce-scatter.9.cloned.1.call-start = ((), (), s32[]{:S(2)}) async-start(), calls=%async_computation.11 | async-start | bytes 7864320 | tf_op jit(solution)/shard_map/reduce_scatter | solution.py:210
  520.5 111.7 %all-gather.17.cloned.1.call-start = ((), (), s32[]{:S(2)}) async-start(), calls=%async_computation.12 | async-start | bytes 7864320 | tf_op jit(solution)/shard_map/all_gather | solution.py:222
  578.8 3.6 copy-start.4
  578.9 3.8 copy-start.10
  578.9 3.8 copy-start.25
  582.6 49.6 %copy-start.14 = (bf16[192,768]{0,1:T(8,128)(2,1)S(1)}, bf16[192,768]{0,1:T(8,128)(2,1)}, u32[]{:S(2)}) copy-start(bf16[192,768]{0,1:T(8,128)(2,1)} %copy-done.13) | copy-start | bytes 884740
  585.6 251.8 %reduce-scatter.11.cloned.1.call-start = ((), (), s32[]{:S(2)}) async-start(), calls=%async_computation.13 | async-start | bytes 7864320 | tf_op jit(solution)/shard_map/reduce_scatter | solution.py:271
  737.5 1.0 copy-start.18
  738.5 6.4 copy-start.9
  744.9 1.5 copy-start.29
  745.8 1.4 copy-start.8
  747.2 1.5 copy-start.16
  748.7 6.4 copy-start.22
  755.1 8.0 copy-start.12
  779.1 0.9 copy-start.20
Sparse Core Ops, SparseCore 0:
  10.4 49.0 all-gather.6
  220.5 59.2 reduce-scatter.4
  453.9 46.3 all-gather.14
  585.8 46.3 all-gather.16
Sparse Core Ops, SparseCore 1:
  223.0 42.4 all-gather.10
  285.0 46.2 all-gather.8
  333.6 41.5 all-gather.12
  388.1 56.7 reduce-scatter.6
  520.6 58.2 reduce-scatter.8
  779.2 58.2 reduce-scatter.10
where the time goes:
time: 861 us; the launch traced here: 849 us
  waiting for transfers between devices  343 us (40%)
  matrix products  224 us (26%)
  blocking collectives  165 us (19%)
  other arithmetic  56.9 us (7%)
  local copies, waits for them, and re-layouts  43 us (5%)
  between operations  16.2 us (2%)
    reduce_scatter x1, waiting for transfers between devices, body(): lax.psum_scatter(jnp.dot(context, full_out, preferred_element_type=wide_m...  58.8 us
    reduce_scatter x1, waiting for transfers between devices, body(): lax.psum_scatter(jnp.einsum('rf,df->rd', grad_inner, full_up, preferred_e...  58.3 us
    reduce_scatter x1, waiting for transfers between devices, body(): lax.psum_scatter(jnp.dot(active, full_down, preferred_element_type=wide_m...  56.7 us
    all_gather x1, waiting for transfers between devices, body(): grad_gathered = lax.all_gather(grad_branch, 'tensor', axis=0, tiled=True)  46.5 us
    all_gather x1, waiting for transfers between devices, body(): lax.all_gather(grad_attn, 'tensor', axis=0, tiled=True)  46.5 us
    all_gather x1, waiting for transfers between devices, body(): lax.all_gather(middle, 'tensor', axis=0, tiled=True)  45.7 us
    psum x1, blocking collectives, body(): grad_lq, grad_lv = lax.psum((grad_lq, grad_lv), 'dp')  37.7 us
    dot_general x1, matrix products, body(): jnp.dot(lax.all_gather(middle, 'tensor', axis=0, tiled=True), full_up, pr...  34 us
  transfers between devices with their start and end apart: 10, of which 8 were waited for; matrix products, arithmetic and copies ran while one was open for 5% of the time, Pallas kernels for 0%

commit v1 on v0

v1 whole, which is shorter than its diff:
```python
import jax
import jax.numpy as jnp
from jax import lax
from jax.sharding import PartitionSpec as P

HEAD_DIM = 64
ADAPTER_RANK = 8
ADAPTER_NUMER = 16
SEQ = 512
EPSILON = 1e-05
NEG_FILL = -1e30
WIDE = jnp.float32
NARROW = jnp.bfloat16


def layer_norm(rows, gain, shift):
    mean = jnp.mean(rows, axis=-1, keepdims=True)
    centered = rows - mean
    variance = jnp.mean(centered * centered, axis=-1, keepdims=True)
    inverse = lax.rsqrt(variance + EPSILON)
    normed = centered * inverse
    return normed * gain + shift, normed, inverse


def norm_back(grad, normed, inverse, gain):
    scaled = grad * gain
    centered = scaled - jnp.mean(scaled, axis=-1, keepdims=True)
    return inverse * (centered - normed * jnp.mean(scaled * normed, axis=-1, keepdims=True))


def mm(left, right):
    return jnp.dot(left, right, preferred_element_type=WIDE)


def mm_nt(left, right):
    return lax.dot_general(left, right, (((1,), (1,)), ((), ())), preferred_element_type=WIDE)


def mm_tn(left, right):
    return lax.dot_general(left, right, (((0,), (0,)), ((), ())), preferred_element_type=WIDE)


def body(
    layer_input_rows,
    output_gradient,
    query_weight,
    key_weight,
    value_weight,
    output_weight,
    up_weight,
    down_weight,
    query_bias_vector,
    value_bias_vector,
    output_bias_vector,
    up_bias_vector,
    down_bias_vector,
    query_down_frozen,
    value_down_frozen,
    query_up_trained,
    value_up_trained,
    first_norm_gain,
    first_norm_bias,
    second_norm_gain,
    second_norm_bias,
    segments,
    sentence_row_mask,
):
    adapter_scale = ADAPTER_NUMER / ADAPTER_RANK
    everyone = ("tensor", "dp")

    def spread(block):
        return lax.all_gather(block, everyone, axis=0, tiled=True)

    width = layer_input_rows.shape[1]
    rows = layer_input_rows.shape[0]

    def columns(block):
        full = spread(block)
        groups = full.shape[0] // width
        return full.reshape(groups, width, block.shape[1]).transpose(1, 0, 2).reshape(width, -1)

    full_query = columns(query_weight)
    full_key = columns(key_weight)
    full_value = columns(value_weight)
    full_out_t = columns(output_weight.T)
    full_up = columns(up_weight)
    full_down_t = columns(down_weight.T)
    query_bias = lax.all_gather(query_bias_vector, "tensor", axis=0, tiled=True)
    value_bias = lax.all_gather(value_bias_vector, "tensor", axis=0, tiled=True)
    up_bias = lax.all_gather(up_bias_vector, "tensor", axis=0, tiled=True)
    query_up = lax.all_gather(query_up_trained, "tensor", axis=1, tiled=True)
    value_up = lax.all_gather(value_up_trained, "tensor", axis=1, tiled=True)

    place = lax.axis_index("tensor")
    segment_ids = lax.dynamic_slice_in_dim(segments, place * rows, rows).reshape(-1, SEQ)
    live = lax.dynamic_slice_in_dim(sentence_row_mask, place * rows, rows).reshape(-1, SEQ)
    seqs = rows // SEQ
    heads = width // HEAD_DIM

    x = layer_input_rows
    u_q = mm(x, query_down_frozen).astype(NARROW)
    u_v = mm(x, value_down_frozen).astype(NARROW)
    q = (mm(x, full_query) + query_bias + adapter_scale * mm(u_q, query_up)).astype(NARROW)
    k = mm(x, full_key).astype(NARROW)
    v = (mm(x, full_value) + value_bias + adapter_scale * mm(u_v, value_up)).astype(NARROW)

    def by_heads(block):
        return block.reshape(seqs, SEQ, heads, HEAD_DIM)

    scale = HEAD_DIM**-0.5
    qh, kh, vh = by_heads(q), by_heads(k), by_heads(v)
    places = jnp.arange(SEQ)
    allowed = (segment_ids[:, :, None] == segment_ids[:, None, :]) & (live[:, None, :] == 1)
    allowed = allowed | (places[:, None] == places[None, :])[None]
    scores = jnp.einsum("sqhd,skhd->shqk", qh, kh, preferred_element_type=WIDE) * scale
    scores = jnp.where(allowed[:, None], scores, NEG_FILL)
    highest = jnp.max(scores, axis=-1, keepdims=True)
    powers = jnp.exp(scores - highest)
    probs = (powers / jnp.sum(powers, axis=-1, keepdims=True)).astype(NARROW)
    context = (
        jnp.einsum("shqk,skhd->sqhd", probs, vh, preferred_element_type=WIDE)
        .astype(NARROW)
        .reshape(rows, width)
    )
    attn = mm_nt(context, full_out_t) + output_bias_vector
    first, n1, s1 = layer_norm(x.astype(WIDE) + attn, first_norm_gain, first_norm_bias)
    middle = first.astype(NARROW)
    inner = mm(middle, full_up) + up_bias
    active, slope = jax.vjp(lambda value: jax.nn.gelu(value, approximate=False), inner)
    ffn = mm_nt(active.astype(NARROW), full_down_t) + down_bias_vector
    output, n2, s2 = layer_norm(first + ffn, second_norm_gain, second_norm_bias)

    grad_second = norm_back(output_gradient.astype(WIDE), n2, s2, second_norm_gain)
    grad_active = mm(grad_second.astype(NARROW), full_down_t)
    grad_inner = slope(grad_active)[0].astype(NARROW)
    grad_first = norm_back(grad_second + mm_nt(grad_inner, full_up), n1, s1, first_norm_gain)
    grad_context = by_heads(mm(grad_first.astype(NARROW), full_out_t).astype(NARROW))
    grad_probs = jnp.einsum("sqhd,skhd->shqk", grad_context, vh, preferred_element_type=WIDE)
    probs_wide = probs.astype(WIDE)
    inside = jnp.sum(probs_wide * grad_probs, axis=-1, keepdims=True)
    grad_scores = (probs_wide * (grad_probs - inside)).astype(NARROW)
    gq = jnp.einsum("shqk,skhd->sqhd", grad_scores, kh, preferred_element_type=WIDE) * scale
    gk = jnp.einsum("shqk,sqhd->skhd", grad_scores, qh, preferred_element_type=WIDE) * scale
    gv = jnp.einsum("shqk,sqhd->skhd", probs, grad_context, preferred_element_type=WIDE)
    gq, gk, gv = (item.astype(NARROW).reshape(rows, width) for item in (gq, gk, gv))
    back_q = adapter_scale * mm_nt(gq, query_up)
    back_v = adapter_scale * mm_nt(gv, value_up)
    grad_input = (
        grad_first
        + mm_nt(gq, full_query)
        + mm_nt(gk, full_key)
        + mm_nt(gv, full_value)
        + mm_nt(back_q, query_down_frozen.astype(WIDE))
        + mm_nt(back_v, value_down_frozen.astype(WIDE))
    )
    grads = jnp.concatenate([mm_tn(u_q, gq), mm_tn(u_v, gv)], axis=0) * adapter_scale
    grads = lax.psum(grads, everyone)
    mine = query_up_trained.shape[1]
    grads = lax.dynamic_slice_in_dim(grads, place * mine, mine, axis=1)
    return (
        output.astype(NARROW),
        grad_input.astype(NARROW),
        grads[:ADAPTER_RANK],
        grads[ADAPTER_RANK:],
    )


IN_SPECS = (
    P(("dp", "tensor"), None),
    P(("dp", "tensor"), None),
    P("dp", "tensor"),
    P("dp", "tensor"),
    P("dp", "tensor"),
    P("tensor", "dp"),
    P("dp", "tensor"),
    P("tensor", "dp"),
    P("tensor"),
    P("tensor"),
    P(),
    P("tensor"),
    P(),
    P(),
    P(),
    P(None, "tensor"),
    P(None, "tensor"),
    P(),
    P(),
    P(),
    P(),
    P("dp"),
    P("dp"),
)
OUT_SPECS = (
    P(("dp", "tensor"), None),
    P(("dp", "tensor"), None),
    P(None, "tensor"),
    P(None, "tensor"),
)


def solution(mesh):
    return jax.shard_map(body, mesh=mesh, in_specs=IN_SPECS, out_specs=OUT_SPECS, check_vma=False)
```

time: 861 us -> 619 us (0.72)
  blocking collectives: 165 us -> 64.1 us
  waiting for transfers between devices: 343 us -> 244 us
  matrix products: 224 us -> 167 us
  local copies, waits for them, and re-layouts: 43 us -> 82.3 us
  other arithmetic: 56.9 us -> 36 us
    reduce_scatter x4 -> x0, waiting for transfers between devices: 193 us -> none  [the longest x1 58.8 us: body(): lax.psum_scatter(jnp.dot(context, full_out, preferred_element_type=wide_m...]
    all_gather x4 -> x3, blocking collectives: 127 us -> 16.7 us  [the longest x1 6.18 us: body(): query_up = lax.all_gather(query_up_trained, 'tensor', axis=1, tiled=True)]
    all_gather x6, waiting for transfers between devices: 149 us -> 241 us  [spread(): return lax.all_gather(block, everyone, axis=0, tiled=True)]
    dot_general x75 -> x24, matrix products: 224 us -> 153 us  [the longest x8 66.8 us: mm_nt(): lax.dot_general(left, right, (((1,), (1,)), ((), ())), preferred_element_...]
    reshape x2 -> x8, local copies, waits for them, and re-layouts: 2.64 us -> 25.1 us  [the longest x4 12.6 us: columns(): full.reshape(groups, width, block.shape[1]).transpose(1, 0, 2)]
    convert_element_type x0 -> x8, local copies, waits for them, and re-layouts: none -> 16.7 us  [the longest x3 6.36 us: body(): item.astype(NARROW).reshape(rows, width)]
    transpose x0 -> x6, local copies, waits for them, and re-layouts: none -> 16.4 us  [columns(): full.reshape(groups, width, block.shape[1]).transpose(1, 0, 2)]
    sub x0 -> x1, matrix products: none -> 14.8 us  [body(): powers = jnp.exp(scores - highest)]
  transfers between devices with their start and end apart: 10 -> 6, of which waited for: 8 -> 6; matrix products, arithmetic and copies ran while one was open for 5% -> 15% of each run, Pallas kernels for 0% -> 0%
where the time goes in v1:
time: 619 us; the launch traced here: 610 us
  waiting for transfers between devices  244 us (39%)
  matrix products  167 us (27%)
  local copies, waits for them, and re-layouts  82.3 us (13%)
  blocking collectives  64.1 us (10%)
  other arithmetic  36 us (6%)
  between operations  15.8 us (3%)
    all_gather x6, waiting for transfers between devices, spread(): return lax.all_gather(block, everyone, axis=0, tiled=True)  241 us
    dot_general x8, matrix products, mm_nt(): lax.dot_general(left, right, (((1,), (1,)), ((), ())), preferred_element_...  66.8 us
    dot_general x9, matrix products, mm(): return jnp.dot(left, right, preferred_element_type=WIDE)  49.7 us
    psum x1, blocking collectives, body(): grads = lax.psum(grads, everyone)  40 us
    unnamed x99, local copies, waits for them, and re-layouts  22.7 us
    convert_element_type x1, other arithmetic, body(): grad_scores = (probs_wide * (grad_probs - inside)).astype(NARROW)  17.1 us
    transpose x6, local copies, waits for them, and re-layouts, columns(): full.reshape(groups, width, block.shape[1]).transpose(1, 0, 2)  16.4 us
    sub x1, matrix products, body(): powers = jnp.exp(scores - highest)  14.8 us
  transfers between devices with their start and end apart: 6, of which 6 were waited for; matrix products, arithmetic and copies ran while one was open for 15% of the time, Pallas kernels for 0%

profile of v1, /device:TPU:0, one launch (start us, length us, event | category | flops | bytes accessed | tf_op | source)
XLA Modules:
  0.0 609.7 jit_solution(543538263132884549)
XLA Ops:
  9.5 1.5 copy.136
  12.2 2.6 copy.141
  16.2 6.2 %all-gather.1 = bf16[4,192,8]{1,2,0:T(8,128)(2,1)S(1)} all-gather(bf16[1,192,8]{1,2,0:T(8,128)(2,1)S(1)} %bitcast.150), channel_id=1, replica_groups=mesh['dp'=8,'tensor'=4] {'tensor'}, dimensions={0}, use_global_device_ids=true | all-gather | bytes 15360 | tf_op jit(solution)/shard_map/all_gather | solution.py:91
  22.5 5.4 all-gather
  28.0 1.6 copy.119
  31.4 7.4 %all-reduce.2 = (f32[768]{0:T(1024)S(1)}, f32[768]{0:T(1024)S(1)}) all-reduce(f32[768]{0:T(1024)S(1)} %dynamic-update-slice.1, f32[768]{0:T(1024)S(1)} %dynamic-update-slice), channel_id=1, replica_groups=mesh['dp'=8,'tensor'=4] {'tensor'}, use_global_device_ids=true, to_apply=%add.1 | all-reduce | flops 1536 | bytes 12288
  38.8 5.2 all-gather.2
  44.0 1.4 and_or_fusion
  46.4 22.4 %all-gather.14.cloned.1.call-done = bf16[3072,192]{1,0:T(8,128)(2,1)} async-done(((bf16[96,192]{1,0:T(8,128)(2,1)}), bf16[3072,192]{1,0:T(8,128)(2,1)}) %all-gather.14.cloned.1.call-update) | async-done | bytes 1179664 | tf_op jit(solution)/shard_map/all_gather | solution.py:72
  68.8 2.7 copy.172
  72.7 1.4 convolution_convert_fusion.3
  74.1 1.6 copy.130
  75.8 2.9 reshape.154
  78.7 47.1 %all-gather.12.cloned.1.call-done = bf16[3072,192]{1,0:T(8,128)(2,1)} async-done(((bf16[96,192]{1,0:T(8,128)(2,1)}), bf16[3072,192]{1,0:T(8,128)(2,1)}) %all-gather.12.cloned.1.call-update) | async-done | bytes 1179664 | tf_op jit(solution)/shard_map/all_gather | solution.py:72
  125.7 3.6 copy.171
  129.3 1.4 copy.125
  130.7 1.4 fusion.83
  132.2 1.8 add_convert_fusion.4
  133.9 2.6 copy.127
  136.5 3.8 reshape.151
  140.4 42.3 %all-gather.10.cloned.1.call-done = bf16[3072,192]{1,0:T(8,128)(2,1)} async-done(((bf16[96,192]{1,0:T(8,128)(2,1)}), bf16[3072,192]{1,0:T(8,128)(2,1)}) %all-gather.10.cloned.1.call-update) | async-done | bytes 1179664 | tf_op jit(solution)/shard_map/all_gather | solution.py:72
  182.7 3.6 copy.170
  186.3 1.4 copy.121
  187.7 1.4 fusion.82
  189.8 1.7 copy.123
  191.4 2.9 reshape.148
  194.4 14.8 %fusion.69 = (f32[2,12,512]{2,1,0:T(8,128)S(1)}, f32[2,12,512,512]{2,3,1,0:T(8,128)}) fusion(pred[2,512,512]{1,2,0:T(8,128)(4,1)} %and_or_fusion, bf16[2,512,12,64]{1,0,3,2:T(2,128)(2,1)S(1)} %reshape.154, bf16[2,512,12,64]{1,0,3,2:T(2,128)(2,1)} %reshape.151), kind=kOutput, calls=%fused_computation.113 | convolution fusion | flops 830472704 | bytes 28884992 | tf_op jit(solution)/shard_map/sub | solution.py:118
  209.1 10.2 %divide_convert_fusion = bf16[2,12,512,512]{2,3,1,0:T(8,128)(2,1)S(1)} fusion(f32[2,12,512,512]{2,3,1,0:T(8,128)} %get-tuple-element.30, f32[2,12,512]{2,1,0:T(8,128)S(1)} %get-tuple-element.29), kind=kLoop, calls=%fused_computation.5 | loop fusion | flops 12582912 | bytes 37797888 | tf_op jit(solution)/shard_map/convert_element_type | solution.py:119
  219.4 2.0 fusion.30
  221.4 2.5 copy-done.1
  223.8 1.6 copy.135
  225.5 1.6 copy.174
  227.0 12.4 %all-gather.16.cloned.1.call-done = bf16[3072,192]{1,0:T(8,128)(2,1)} async-done(((bf16[96,192]{1,0:T(8,128)(2,1)}), bf16[3072,192]{1,0:T(8,128)(2,1)}) %all-gather.16.cloned.1.call-update) | async-done | bytes 1179664 | tf_op jit(solution)/shard_map/all_gather | solution.py:72
  239.4 2.7 copy.173
  242.3 4.0 fusion.78
  246.7 58.1 %all-gather.20.cloned.1.call-done = bf16[3072,768]{1,0:T(8,128)(2,1)} async-done(((bf16[96,768]{1,0:T(8,128)(2,1)}), bf16[3072,768]{1,0:T(8,128)(2,1)}) %all-gather.20.cloned.1.call-update) | async-done | bytes 4718608 | tf_op jit(solution)/shard_map/all_gather | solution.py:72
  304.8 6.7 %copy.140 = bf16[768,4,768]{0,2,1:T(8,128)(2,1)} copy(bf16[768,4,768]{2,0,1:T(8,128)(2,1)} %bitcast.121) | data formatting | bytes 9437184 | tf_op jit(solution)/shard_map/transpose | solution.py:80
  311.4 58.6 %all-gather.18.cloned.1.call-done = bf16[3072,768]{1,0:T(8,128)(2,1)} async-done(((bf16[96,768]{1,0:T(8,128)(2,1)}), bf16[3072,768]{1,0:T(8,128)(2,1)}) %all-gather.18.cloned.1.call-update) | async-done | bytes 4718608 | tf_op jit(solution)/shard_map/all_gather | solution.py:72
  370.0 6.7 %copy.139 = bf16[768,4,768]{0,2,1:T(8,128)(2,1)} copy(bf16[768,4,768]{2,0,1:T(8,128)(2,1)} %bitcast.122) | data formatting | bytes 9437184 | tf_op jit(solution)/shard_map/transpose | solution.py:80
  376.7 36.4 %fusion.4 = (f32[1024,3072]{1,0:T(8,128)}, f32[1024,3072]{1,0:T(8,128)}) fusion(f32[3072]{0:T(1024)S(1)} %bitcast.147, bf16[768,3072]{0,1:T(8,128)(2,1)} %bitcast.125, f32[1024,768]{0,1:T(8,128)S(1)} %get-tuple-element.32, f32[768]{0:T(1024)S(1)} %copy-done.38, f32[768]{0:T(1024)S(1)} %copy-done.39, f32[1024]{0:T(1024)S(1)} %add_rsqrt_fusion.1, ...), kind=kOutput, calls=%fused_computation.10 | convolution fusion | flops 5033951232 | bytes 33056768 | tf_op jit(solution)/shard_map/dot_general | solution.py:32
  413.2 17.1 %fusion.79 = (f32[1024]{0:T(1024)S(1)}, f32[1024,768]{0,1:T(8,128)}) fusion(f32[768]{0:T(1024)S(1)} %copy-done.37, bf16[768,3072]{0,1:T(8,128)(2,1)} %bitcast.123, f32[1024,3072]{1,0:T(8,128)} %get-tuple-element.33, f32[1024,3072]{1,0:T(8,128)} %get-tuple-element.34, f32[3072]{0:T(1024)S(1)} %bitcast.148, f32[768]{0:T(1024)S(1)} %copy-done.38, ...), kind=kOutput, calls=%fused_computation.115 | convolution fusion | flops 4849925120 | bytes 36209664 | tf_op jit(solution)/shard_map/dot_general | solution.py:36
  430.3 2.4 multiply_reduce_fusion.2
  433.1 3.7 fusion.19
  436.8 25.1 %fusion.67 = (f32[1024]{0:T(1024)S(1)}, f32[1024]{0:T(1024)S(1)}, f32[1024,768]{0,1:T(8,128)}) fusion(f32[1024]{0:T(1024)S(1)} %add_rsqrt_fusion.1, f32[1024,768]{0,1:T(8,128)S(1)} %get-tuple-element.32, f32[1024]{0:T(1024)S(1)} %broadcast_multiply_fusion.5, f32[768]{0:T(1024)S(1)} %copy-done.39, bf16[768,3072]{0,1:T(8,128)(2,1)} %bitcast.126, ...), kind=kOutput, calls=%fused_computation.111 | convolution fusion | flops 9729734656 | bytes 45664256 | tf_op jit(solution)/shard_map/dot_general | solution.py:36
  462.0 5.5 convolution_convert_fusion.2
  467.5 2.8 copy.142
  470.3 2.9 reshape.162
  473.2 12.9 %fusion.1 = (f32[2,12,512]{2,1,0:T(8,128)S(1)}, f32[2,12,512,512]{2,3,1,0:T(8,128)}) fusion(bf16[2,12,512,512]{2,3,1,0:T(8,128)(2,1)} %copy-done.1, bf16[2,512,12,64]{1,0,3,2:T(2,128)(2,1)S(1)} %copy-done.4, bf16[2,512,12,64]{1,0,3,2:T(2,128)(2,1)S(1)} %reshape.162), kind=kOutput, calls=%fused_computation.3 | convolution fusion | flops 824168448 | bytes 40943616 | tf_op jit(solution)/shard_map/sqhd,skhd->shqk/dot_general | solution.py:138
  486.1 8.5 %fusion.31 = bf16[2,512,12,64]{1,3,2,0:T(8,128)(2,1)S(1)} fusion(bf16[2,12,512,512]{2,3,1,0:T(8,128)(2,1)} %copy-done.1, bf16[2,512,12,64]{1,0,3,2:T(2,128)(2,1)S(1)} %reshape.162), kind=kOutput, calls=%fused_computation.69 | convolution fusion | flops 806092800 | bytes 15728640 | tf_op jit(solution)/shard_map/shqk,sqhd->skhd/dot_general | solution.py:144
  494.6 17.1 %fusion.2 = bf16[2,12,512,512]{2,3,1,0:T(8,128)(2,1)S(1)} fusion(f32[2,12,512,512]{2,3,1,0:T(8,128)} %get-tuple-element.39, f32[2,12,512]{2,1,0:T(8,128)S(1)} %get-tuple-element.38, f32[2,12,512,512]{2,3,1,0:T(8,128)} %get-tuple-element.30, f32[2,12,512]{2,1,0:T(8,128)S(1)} %copy-done.18), kind=kLoop, calls=%fused_computation.4 | loop fusion | flops 37748736 | bytes 63012864 | tf_op jit(solution)/shard_map/convert_element_type | solution.py:141
  511.7 4.5 copy-done.2
  516.2 2.1 fusion.32
  518.4 9.6 %fusion.33 = bf16[2,512,12,64]{1,3,2,0:T(8,128)(2,1)} fusion(bf16[2,12,512,512]{2,3,1,0:T(8,128)(2,1)} %copy-done.2, bf16[2,512,12,64]{1,0,3,2:T(2,128)(2,1)S(1)} %copy-done.10), kind=kOutput, calls=%fused_computation.71 | convolution fusion | flops 806879232 | bytes 15728640 | tf_op jit(solution)/shard_map/shqk,sqhd->skhd/dot_general | solution.py:143
  528.0 1.6 copy.147
  530.1 2.5 fusion.52
  532.5 4.4 fusion.84
  536.9 1.6 copy.155
  539.0 3.2 fusion.86
  543.2 2.8 copy.159
  546.0 3.1 copy.151
  549.6 3.1 fusion.85
  552.7 7.4 %add_convert_fusion.2 = bf16[1024,768]{0,1:T(8,128)(2,1)S(1)} fusion(f32[1024,768]{0,1:T(8,128)} %fusion.52, f32[1024,768]{0,1:T(8,128)} %fusion.86, f32[1024,768]{0,1:T(8,128)} %fusion.85, f32[1024,768]{0,1:T(8,128)} %fusion.84, bf16[768,8]{0,1:T(8,128)(2,1)S(1)} %copy-done.28, bf16[1024,768]{0,1:T(8,128)(2,1)S(1)} %bitcast.113, ...), kind=kOutput, calls=%fused_computation.34 | convolution fusion | flops 34611200 | bytes 22061056 | tf_op jit(solution)/shard_map/dot_general | solution.py:36
  560.2 1.6 copy.160
  561.7 40.0 %psum.7 = f32[16,768]{1,0:T(8,128)S(1)} all-reduce(f32[16,768]{1,0:T(8,128)S(1)} %maximum_multiply_fusion), channel_id=1, replica_groups=mesh['dp'=8,'tensor'=4] {'tensor','dp'}, use_global_device_ids=true, to_apply=%region_11.12 | all-reduce | flops 12288 | bytes 98304 | tf_op jit(solution)/shard_map/psum | solution.py:157
  (127 shorter events, 12.9 us)
Async XLA Ops:
  7.2 38.2 %copy-start = (bf16[768,8]{0,1:T(8,128)(2,1)S(1)}, bf16[768,8]{0,1:T(8,128)(2,1)}, u32[]{:S(2)}) copy-start(bf16[768,8]{0,1:T(8,128)(2,1)} %param.36) | copy-start | bytes 36868
  7.2 7.6 %copy-start.33 = (f32[768]{0:T(1024)S(1)}, f32[768]{0:T(1024)}, u32[]{:S(2)}) copy-start(f32[768]{0:T(1024)} %param.34) | copy-start | bytes 9220
  7.2 9.0 %copy-start.31 = (bf16[8,192]{1,0:T(8,128)(2,1)S(1)}, bf16[8,192]{1,0:T(8,128)(2,1)}, u32[]{:S(2)}) copy-start(bf16[8,192]{1,0:T(8,128)(2,1)} %param.38) | copy-start | bytes 9220
  7.2 15.3 %copy-start.32 = (bf16[8,192]{1,0:T(8,128)(2,1)S(1)}, bf16[8,192]{1,0:T(8,128)(2,1)}, u32[]{:S(2)}) copy-start(bf16[8,192]{1,0:T(8,128)(2,1)} %param.39) | copy-start | bytes 9220
  7.2 20.8 %copy-start.5 = (bf16[1024,768]{1,0:T(8,128)(2,1)S(1)}, bf16[1024,768]{1,0:T(8,128)(2,1)}, u32[]{:S(2)}) copy-start(bf16[1024,768]{1,0:T(8,128)(2,1)} %param.23) | copy-start | bytes 4718596
  7.2 61.6 %all-gather.14.cloned.1.call-start = ((), (), s32[]{:S(2)}) async-start(), calls=%async_computation.2 | async-start | bytes 1622016 | tf_op jit(solution)/shard_map/all_gather | solution.py:72
  8.0 117.8 %all-gather.12.cloned.1.call-start = ((), (), s32[]{:S(2)}) async-start(), calls=%async_computation.1 | async-start | bytes 1622016 | tf_op jit(solution)/shard_map/all_gather | solution.py:72
  8.7 173.9 %all-gather.10.cloned.1.call-start = ((), (), s32[]{:S(2)}) async-start(), calls=%async_computation | async-start | bytes 1622016 | tf_op jit(solution)/shard_map/all_gather | solution.py:72
  9.4 230.0 %all-gather.16.cloned.1.call-start = ((), (), s32[]{:S(2)}) async-start(), calls=%async_computation.3 | async-start | bytes 1622016 | tf_op jit(solution)/shard_map/all_gather | solution.py:72
  11.0 293.8 %all-gather.20.cloned.1.call-start = ((), (), s32[]{:S(2)}) async-start(), calls=%async_computation.5 | async-start | bytes 4866048 | tf_op jit(solution)/shard_map/all_gather | solution.py:72
  11.6 358.4 %all-gather.18.cloned.1.call-start = ((), (), s32[]{:S(2)}) async-start(), calls=%async_computation.4 | async-start | bytes 4866048 | tf_op jit(solution)/shard_map/all_gather | solution.py:72
  12.2 17.5 %copy-start.40 = (u32[32]{0:T(128)S(1)}, u32[32]{0:T(128)}, u32[]{:S(2)}) copy-start(u32[32]{0:T(128)} %constant.103) | copy-start | bytes 388
  12.2 18.7 %copy-start.34 = (f32[192]{0:T(256)S(1)}, f32[192]{0:T(256)}, u32[]{:S(2)}) copy-start(f32[192]{0:T(256)} %param.31) | copy-start | bytes 2308
  12.2 18.9 %copy-start.35 = (f32[192]{0:T(256)S(1)}, f32[192]{0:T(256)}, u32[]{:S(2)}) copy-start(f32[192]{0:T(256)} %param.32) | copy-start | bytes 2308
  14.8 31.1 %copy-start.27 = (bf16[768,8]{0,1:T(8,128)(2,1)S(1)}, bf16[768,8]{0,1:T(8,128)(2,1)}, u32[]{:S(2)}) copy-start(bf16[768,8]{0,1:T(8,128)(2,1)} %param.37) | copy-start | bytes 36868
  22.5 109.6 %copy-start.25 = (bf16[768,8]{0,1:T(8,128)(2,1)}, bf16[768,8]{0,1:T(8,128)(2,1)S(1)}, u32[]{:S(2)}) copy-start(bf16[768,8]{0,1:T(8,128)(2,1)S(1)} %reshape.175) | copy-start | bytes 36868
  28.0 161.1 %copy-start.23 = (bf16[768,8]{0,1:T(8,128)(2,1)}, bf16[768,8]{0,1:T(8,128)(2,1)S(1)}, u32[]{:S(2)}) copy-start(bf16[768,8]{0,1:T(8,128)(2,1)S(1)} %reshape.173) | copy-start | bytes 36868
  45.9 86.3 %copy-start.19 = (bf16[1024,8]{0,1:T(8,128)(2,1)}, bf16[1024,8]{0,1:T(8,128)(2,1)S(1)}, u32[]{:S(2)}) copy-start(bf16[1024,8]{0,1:T(8,128)(2,1)S(1)} %convolution_convert_fusion.4) | copy-start | bytes 49156
  46.4 142.7 %copy-start.21 = (bf16[1024,8]{0,1:T(8,128)(2,1)}, bf16[1024,8]{0,1:T(8,128)(2,1)S(1)}, u32[]{:S(2)}) copy-start(bf16[1024,8]{0,1:T(8,128)(2,1)S(1)} %convolution_convert_fusion.5) | copy-start | bytes 49156
  71.7 1.0 copy-start.11
  78.6 115.7 %copy-start.8 = (bf16[2,512,12,64]{1,0,3,2:T(2,128)(2,1)}, bf16[2,512,12,64]{1,0,3,2:T(2,128)(2,1)S(1)}, u32[]{:S(2)}) copy-start(bf16[2,512,12,64]{1,0,3,2:T(2,128)(2,1)S(1)} %reshape.154) | copy-start | bytes 4718596
  130.7 1.4 copy-start.13
  187.6 1.4 copy-start.14
  194.3 25.0 %copy-start.3 = (bf16[2,512,12,64]{1,0,3,2:T(2,128)(2,1)}, bf16[2,512,12,64]{1,0,3,2:T(2,128)(2,1)S(1)}, u32[]{:S(2)}) copy-start(bf16[2,512,12,64]{1,0,3,2:T(2,128)(2,1)S(1)} %reshape.148) | copy-start | bytes 4718596
  209.1 10.2 %copy-start.17 = (f32[2,12,512]{2,1,0:T(8,128)}, f32[2,12,512]{2,1,0:T(8,128)S(1)}, u32[]{:S(2)}) copy-start(f32[2,12,512]{2,1,0:T(8,128)S(1)} %get-tuple-element.29) | copy-start | bytes 147460
  219.4 4.5 copy-start.1
  227.0 15.3 %copy-start.36 = (f32[768]{0:T(1024)S(1)}, f32[768]{0:T(1024)}, u32[]{:S(2)}) copy-start(f32[768]{0:T(1024)} %param.33) | copy-start | bytes 9220
  242.3 4.0 copy-start.16
  246.3 215.7 %copy-start.6 = (f32[1024,768]{0,1:T(8,128)}, f32[1024,768]{0,1:T(8,128)S(1)}, u32[]{:S(2)}) copy-start(f32[1024,768]{0,1:T(8,128)S(1)} %get-tuple-element.32) | copy-start | bytes 9437188
  370.0 6.7 %copy-start.38 = (f32[768]{0:T(1024)S(1)}, f32[768]{0:T(1024)}, u32[]{:S(2)}) copy-start(f32[768]{0:T(1024)} %param.41) | copy-start | bytes 9220
  370.0 6.7 %copy-start.39 = (f32[768]{0:T(1024)S(1)}, f32[768]{0:T(1024)}, u32[]{:S(2)}) copy-start(f32[768]{0:T(1024)} %param.40) | copy-start | bytes 9220
  376.7 36.5 %copy-start.37 = (f32[768]{0:T(1024)S(1)}, f32[768]{0:T(1024)}, u32[]{:S(2)}) copy-start(f32[768]{0:T(1024)} %param.35) | copy-start | bytes 9220
  430.3 2.8 copy-start.7
  430.3 2.8 copy-start.29
  430.3 2.8 copy-start.30
  467.5 5.7 copy-start.4
  486.1 8.5 %copy-start.18 = (f32[2,12,512]{2,1,0:T(8,128)S(1)}, f32[2,12,512]{2,1,0:T(8,128)}, u32[]{:S(2)}) copy-start(f32[2,12,512]{2,1,0:T(8,128)} %copy-done.17) | copy-start | bytes 147460
  494.6 21.7 %copy-start.9 = (bf16[2,512,12,64]{1,0,3,2:T(2,128)(2,1)S(1)}, bf16[2,512,12,64]{1,0,3,2:T(2,128)(2,1)}, u32[]{:S(2)}) copy-start(bf16[2,512,12,64]{1,0,3,2:T(2,128)(2,1)} %copy-done.8) | copy-start | bytes 4718596
  511.7 4.5 copy-start.2
  516.2 2.2 copy-start.10
  528.0 2.0 copy-start.26
  536.9 2.0 copy-start.15
  539.0 3.2 copy-start.22
  539.0 3.7 copy-start.20
  546.0 3.5 copy-start.12
  549.6 3.2 copy-start.24
  549.6 3.2 copy-start.28
Sparse Core Ops, SparseCore 0:
  11.0 57.8 all-gather.13
  71.7 53.9 all-gather.11
  128.6 53.9 all-gather.9
  185.4 53.9 all-gather.15
  242.2 62.5 all-gather.19
  307.5 62.4 all-gather.17

commit v2 on v1

v2 whole, which is shorter than its diff:
```python
import functools

import jax
import jax.numpy as jnp
from jax import lax
from jax.experimental import pallas as pl
from jax.experimental.pallas import tpu as pltpu
from jax.sharding import PartitionSpec as P

HEAD_DIM = 64
ADAPTER_RANK = 8
ADAPTER_NUMER = 16
SEQ = 512
LANES = 128
EPSILON = 1e-05
NEG_FILL = -1e30
WIDE = jnp.float32
NARROW = jnp.bfloat16
ADAPTER_SCALE = ADAPTER_NUMER / ADAPTER_RANK
SCORE_SCALE = HEAD_DIM**-0.5

KEY_SPANS = ((0, 128), (128, 384), (128, 512), (256, 512))
SPAN_STARTS = (0, 128, 384, 768)
SPAN_TOTAL = 1024


def mm(left, right):
    return jnp.dot(left, right, preferred_element_type=WIDE)


def mm_nt(left, right):
    return lax.dot_general(left, right, (((1,), (1,)), ((), ())), preferred_element_type=WIDE)


def row_mean(block):
    return jnp.sum(block, axis=-1, keepdims=True) * (1.0 / block.shape[-1])


def gelu_parts(value):
    size = jnp.abs(value)
    bell = jnp.exp(value * value * -0.5)
    t = 1.0 / (1.0 + size * (0.3275911 * 0.7071067811865476))
    series = t * (
        0.5 * 0.254829592
        + t
        * (
            0.5 * -0.284496736
            + t * (0.5 * 1.421413741 + t * (0.5 * -1.453152027 + t * (0.5 * 1.061405429)))
        )
    )
    tail = series * bell
    below = jnp.where(value < 0.0, tail, 1.0 - tail)
    return value * below, below + value * bell * 0.3989422804014327


def pair_select(low, high):
    lane = lax.broadcasted_iota(jnp.int32, low.shape, 1)
    return jnp.where(lane < HEAD_DIM, low, pltpu.roll(high, HEAD_DIM, 1))


def kernel(
    x_ref,
    gout_ref,
    a_ref,
    b_ref,
    c_ref,
    vec_ref,
    upb_ref,
    down_t_ref,
    seg_ref,
    live_ref,
    out_ref,
    gin_ref,
    gl_ref,
    wq,
    wk,
    wv,
    wo,
    q,
    k,
    v,
    probs,
    ctx,
    n1,
    s1,
    act,
    slope,
    acc,
    mask,
    u_t,
):
    rows, width = x_ref.shape
    seqs = rows // SEQ
    pairs = width // LANES
    groups = a_ref.shape[0]

    for group in range(groups):
        at = slice(group * LANES, (group + 1) * LANES)
        wq[:, at] = a_ref[group, :, 0:128]
        wk[:, at] = a_ref[group, :, 128:256]
        wv[:, at] = a_ref[group, :, 256:384]
        wo[:, at] = a_ref[group, :, 640:768]
    for half in range(groups // 2):
        at = slice((groups + half) * LANES, (groups + half + 1) * LANES)
        first = a_ref[2 * half, :, 384:512].astype(WIDE)
        second = a_ref[2 * half + 1, :, 384:512].astype(WIDE)
        wq[:, at] = pair_select(first, second).astype(NARROW)
        wk[:, at] = pair_select(pltpu.roll(first, HEAD_DIM, 1), pltpu.roll(second, HEAD_DIM, 1)).astype(NARROW)
        first = a_ref[2 * half, :, 512:640].astype(WIDE)
        second = a_ref[2 * half + 1, :, 512:640].astype(WIDE)
        wv[:, at] = pair_select(first, second).astype(NARROW)
        wo[:, at] = pair_select(pltpu.roll(first, HEAD_DIM, 1), pltpu.roll(second, HEAD_DIM, 1)).astype(NARROW)

    place = lax.broadcasted_iota(jnp.int32, (LANES, LANES), 0) == lax.broadcasted_iota(
        jnp.int32, (LANES, LANES), 1
    )
    for seq in range(seqs):
        wide_ids = []
        key_ids = []
        for block in range(4):
            row = seq * 4 + block
            ids = seg_ref[row : row + 1, :].astype(WIDE)
            live = live_ref[row : row + 1, :]
            key = jnp.where(live == 1, ids, -1.0)
            wide_ids.append(ids)
            key_ids.append(jnp.transpose(jnp.broadcast_to(key, (LANES, LANES))))
        for block in range(1, 4):
            start, stop = KEY_SPANS[block]
            for j in range((stop - start) // LANES):
                kb = start // LANES + j
                seen = key_ids[kb] == wide_ids[block]
                if kb == block:
                    seen = seen | place
                at = SPAN_STARTS[block] + j * LANES
                mask[seq, at : at + LANES, :] = jnp.where(seen, 0.0, NEG_FILL)

    u_t[...] = mm_nt(down_t_ref[...], x_ref[...]).astype(NARROW)

    def project(step, carry):
        at = pl.ds(pl.multiple_of(step * 256, 256), 256)
        xs = x_ref[...]
        q[:, at] = (mm(xs, wq[:, at]) + vec_ref[0:1, at]).astype(NARROW)
        k[:, at] = mm(xs, wk[:, at]).astype(NARROW)
        v[:, at] = (mm(xs, wv[:, at]) + vec_ref[1:2, at]).astype(NARROW)
        return carry

    lax.fori_loop(0, width // 256, project, 0)

    lane = lax.broadcasted_iota(jnp.int32, (LANES, LANES), 1)

    def stacked(tile):
        none = jnp.zeros_like(tile)
        return jnp.concatenate(
            [jnp.where(lane < HEAD_DIM, tile, none), jnp.where(lane < HEAD_DIM, none, tile)], axis=0
        )

    def turned(tile):
        own = jnp.concatenate([tile[:HEAD_DIM, :LANES], tile[HEAD_DIM:, LANES:]], axis=0)
        return jnp.transpose(own)

    def attend(step, carry):
        seq = step // pairs
        pair = step - seq * pairs
        at = pl.ds(pl.multiple_of(pair * LANES, LANES), LANES)
        base = pl.multiple_of(seq * SEQ, SEQ)
        everything = pl.ds(base, SEQ)
        keys = k[everything, at]
        values_t = jnp.transpose(v[everything, at].astype(WIDE)).astype(NARROW)
        for block, (start, stop) in enumerate(KEY_SPANS):
            here = pl.ds(base + block * LANES, LANES)
            scores = mm_nt(keys[start:stop], stacked(q[here, at]))
            span = pl.ds(SPAN_STARTS[block], stop - start)
            if block:
                shade = mask[seq, span, :]
                scores = scores + jnp.concatenate([shade, shade], axis=1)
            top = jnp.max(scores, axis=0, keepdims=True)
            powers = jnp.exp(scores - top)
            total = jnp.sum(powers, axis=0, keepdims=True)
            weights = (powers * (1.0 / total)).astype(NARROW)
            probs[step, span, :] = weights
            ctx[here, at] = turned(mm(values_t[:, start:stop], weights)).astype(NARROW)
        return carry

    lax.fori_loop(0, seqs * pairs, attend, 0)

    def first_norm(step, carry):
        at = pl.ds(pl.multiple_of(step * 256, 256), 256)
        r = x_ref[at, :].astype(WIDE) + (mm_nt(ctx[at, :], wo[...]) + vec_ref[2:3, :])
        centered = r - row_mean(r)
        inverse = lax.rsqrt(row_mean(centered * centered) + EPSILON)
        normed = centered * inverse
        n1[at, :] = normed
        s1[at, :] = inverse
        out_ref[at, :] = (normed * vec_ref[4:5, :] + vec_ref[5:6, :]).astype(NARROW)
        return carry

    lax.fori_loop(0, rows // 256, first_norm, 0)

    def up(group, carry):
        for j in range(width // 256):
            cols = slice(j * 256, (j + 1) * 256)
            at = pl.ds(pl.multiple_of(group * width + j * 256, 256), 256)
            inner = mm(out_ref[...], b_ref[group, :, cols]) + upb_ref[0:1, at]
            value, grad = gelu_parts(inner)
            act[:, at] = value.astype(NARROW)
            slope[:, at] = grad.astype(NARROW)
        return carry

    lax.fori_loop(0, groups, up, 0)

    def second_norm(step, carry):
        at = pl.ds(pl.multiple_of(step * 256, 256), 256)
        r = n1[at, :] * vec_ref[4:5, :] + vec_ref[5:6, :] + vec_ref[3:4, :]
        for group in range(groups):
            r = r + mm_nt(act[at, group * width : (group + 1) * width], c_ref[group])
        centered = r - row_mean(r)
        inverse = lax.rsqrt(row_mean(centered * centered) + EPSILON)
        normed = centered * inverse
        out_ref[at, :] = (normed * vec_ref[6:7, :] + vec_ref[7:8, :]).astype(NARROW)
        e = gout_ref[at, :].astype(WIDE) * vec_ref[6:7, :]
        acc[at, :] = inverse * (e - row_mean(e) - normed * row_mean(e * normed))
        return carry

    lax.fori_loop(0, rows // 256, second_norm, 0)

    def down_back(step, carry):
        at = pl.ds(pl.multiple_of(step * 256, 256), 256)
        second = acc[at, :]
        low = second.astype(NARROW)
        total = second
        for group in range(groups):
            cols = slice(group * width, (group + 1) * width)
            grad = (mm(low, c_ref[group]) * slope[at, cols].astype(WIDE)).astype(NARROW)
            total = total + mm_nt(grad, b_ref[group])
        normed = n1[at, :]
        e = total * vec_ref[4:5, :]
        first = s1[at, :] * (e - row_mean(e) - normed * row_mean(e * normed))
        acc[at, :] = first
        ctx[at, :] = mm(first.astype(NARROW), wo[...]).astype(NARROW)
        return carry

    lax.fori_loop(0, rows // 256, down_back, 0)

    def attend_back(step, carry):
        seq = step // pairs
        pair = step - seq * pairs
        at = pl.ds(pl.multiple_of(pair * LANES, LANES), LANES)
        base = pl.multiple_of(seq * SEQ, SEQ)
        everything = pl.ds(base, SEQ)
        keys = k[everything, at]
        values = v[everything, at]
        keys_t = jnp.transpose(keys.astype(WIDE)).astype(NARROW)
        grad_k = [None] * 4
        grad_v = [None] * 4
        for block, (start, stop) in enumerate(KEY_SPANS):
            here = pl.ds(base + block * LANES, LANES)
            grads = stacked(ctx[here, at])
            span = pl.ds(SPAN_STARTS[block], stop - start)
            weights = probs[step, span, :]
            part = weights.astype(WIDE) * mm_nt(values[start:stop], grads)
            inside = jnp.sum(part, axis=0, keepdims=True)
            grad_scores = (part - weights.astype(WIDE) * inside).astype(NARROW)
            for_keys = mm(grad_scores, stacked(q[here, at]))
            for_values = mm(weights, grads)
            q[here, at] = turned(mm(keys_t[:, start:stop], grad_scores)).astype(NARROW)
            for j in range((stop - start) // LANES):
                kb = start // LANES + j
                rows_here = slice(j * LANES, (j + 1) * LANES)
                grad_k[kb] = for_keys[rows_here] if grad_k[kb] is None else grad_k[kb] + for_keys[rows_here]
                grad_v[kb] = (
                    for_values[rows_here] if grad_v[kb] is None else grad_v[kb] + for_values[rows_here]
                )
        for kb in range(4):
            here = pl.ds(base + kb * LANES, LANES)
            k[here, at] = grad_k[kb].astype(NARROW)
            v[here, at] = grad_v[kb].astype(NARROW)
        return carry

    lax.fori_loop(0, seqs * pairs, attend_back, 0)

    def input_back(step, carry):
        at = pl.ds(pl.multiple_of(step * 256, 256), 256)
        total = acc[at, :] + mm_nt(q[at, :], wq[...])
        total = total + mm_nt(k[at, :], wk[...])
        total = total + mm_nt(v[at, :], wv[...])
        gin_ref[at, :] = total.astype(NARROW)
        return carry

    lax.fori_loop(0, rows // 256, input_back, 0)

    gl_ref[0:8, :] = mm(u_t[0:8, :], q[...]) * (ADAPTER_SCALE * SCORE_SCALE)
    gl_ref[8:16, :] = mm(u_t[8:16, :], v[...]) * ADAPTER_SCALE


def run_layer(x, gout, a, b, c, vectors, up_bias, down_t, seg, live):
    rows, width = x.shape
    hidden = up_bias.shape[1]
    pairs = width // LANES
    seqs = rows // SEQ
    shape = jax.ShapeDtypeStruct
    square = pltpu.VMEM((width, width), NARROW)
    plane = pltpu.VMEM((rows, width), NARROW)
    return pl.pallas_call(
        kernel,
        out_shape=(
            shape((rows, width), NARROW),
            shape((rows, width), NARROW),
            shape((2 * ADAPTER_RANK, width), WIDE),
        ),
        in_specs=[pl.BlockSpec(memory_space=pltpu.VMEM)] * 10,
        out_specs=[pl.BlockSpec(memory_space=pltpu.VMEM)] * 3,
        scratch_shapes=[
            square,
            square,
            square,
            square,
            plane,
            plane,
            plane,
            pltpu.VMEM((seqs * pairs, SPAN_TOTAL, 2 * LANES), NARROW),
            plane,
            pltpu.VMEM((rows, width), WIDE),
            pltpu.VMEM((rows, 1), WIDE),
            pltpu.VMEM((rows, hidden), NARROW),
            pltpu.VMEM((rows, hidden), NARROW),
            pltpu.VMEM((rows, width), WIDE),
            pltpu.VMEM((seqs, SPAN_TOTAL, LANES), WIDE),
            pltpu.VMEM((2 * ADAPTER_RANK, rows), NARROW),
        ],
        compiler_params=pltpu.CompilerParams(vmem_limit_bytes=63 << 20),
    )(x, gout, a, b, c, vectors, up_bias, down_t, seg, live)


def in_pairs(block, groups):
    parts = block.reshape(block.shape[0], groups, 3, HEAD_DIM)
    front = parts[:, :, :2].reshape(block.shape[0], -1)
    return jnp.concatenate([front, parts[:, :, 2].reshape(block.shape[0], -1)], axis=1)


def from_pairs(block, groups):
    front = block[:, : groups * LANES].reshape(block.shape[0], groups, 2, HEAD_DIM)
    back = block[:, groups * LANES :].reshape(block.shape[0], groups, 1, HEAD_DIM)
    return jnp.concatenate([front, back], axis=2).reshape(block.shape[0], -1)


def body(
    layer_input_rows,
    output_gradient,
    query_weight,
    key_weight,
    value_weight,
    output_weight,
    up_weight,
    down_weight,
    query_bias_vector,
    value_bias_vector,
    output_bias_vector,
    up_bias_vector,
    down_bias_vector,
    query_down_frozen,
    value_down_frozen,
    query_up_trained,
    value_up_trained,
    first_norm_gain,
    first_norm_bias,
    second_norm_gain,
    second_norm_bias,
    segments,
    sentence_row_mask,
):
    everyone = ("tensor", "dp")
    rows, width = layer_input_rows.shape
    groups = width // query_weight.shape[1]
    depth = query_weight.shape[0]
    place = lax.axis_index("tensor")
    which = lax.axis_index("dp")

    def folded(weight, down, up):
        own = lax.dynamic_slice_in_dim(down, which * depth, depth, axis=0)
        return weight.astype(WIDE) + ADAPTER_SCALE * mm(own, up)

    wq = (folded(query_weight, query_down_frozen, query_up_trained) * SCORE_SCALE).astype(NARROW)
    wv = folded(value_weight, value_down_frozen, value_up_trained).astype(NARROW)
    wk = key_weight
    wo = output_weight.T
    block_a = jnp.concatenate(
        [wq[:, :128], wk[:, :128], wv[:, :128], wq[:, 128:], wk[:, 128:], wv[:, 128:], wo[:, 128:], wo[:, :128]],
        axis=1,
    )

    def spread(block):
        return lax.all_gather(block, everyone, axis=0, tiled=True).reshape(groups, width, width)

    a, b, c = spread(block_a), spread(up_weight), spread(down_weight.T)
    query_bias = lax.all_gather(query_bias_vector * SCORE_SCALE, "tensor", axis=0, tiled=True)
    value_bias = lax.all_gather(value_bias_vector, "tensor", axis=0, tiled=True)
    up_bias = lax.all_gather(up_bias_vector, "tensor", axis=0, tiled=True)
    vectors = jnp.concatenate(
        [
            in_pairs(query_bias[None], groups),
            in_pairs(value_bias[None], groups),
            output_bias_vector[None],
            down_bias_vector[None],
            first_norm_gain[None],
            first_norm_bias[None],
            second_norm_gain[None],
            second_norm_bias[None],
        ],
        axis=0,
    )
    down_t = jnp.concatenate([query_down_frozen, value_down_frozen], axis=1).T
    seg = lax.dynamic_slice_in_dim(segments, place * rows, rows).reshape(-1, LANES)
    live = lax.dynamic_slice_in_dim(sentence_row_mask, place * rows, rows).reshape(-1, LANES)
    output, grad_input, grads = run_layer(
        layer_input_rows, output_gradient, a, b, c, vectors, up_bias[None], down_t, seg, live
    )
    grads = from_pairs(lax.psum(grads, everyone), groups)
    mine = query_up_trained.shape[1]
    grads = lax.dynamic_slice_in_dim(grads, place * mine, mine, axis=1)
    return output, grad_input, grads[:ADAPTER_RANK], grads[ADAPTER_RANK:]


IN_SPECS = (
    P(("dp", "tensor"), None),
    P(("dp", "tensor"), None),
    P("dp", "tensor"),
    P("dp", "tensor"),
    P("dp", "tensor"),
    P("tensor", "dp"),
    P("dp", "tensor"),
    P("tensor", "dp"),
    P("tensor"),
    P("tensor"),
    P(),
    P("tensor"),
    P(),
    P(),
    P(),
    P(None, "tensor"),
    P(None, "tensor"),
    P(),
    P(),
    P(),
    P(),
    P("dp"),
    P("dp"),
)
OUT_SPECS = (
    P(("dp", "tensor"), None),
    P(("dp", "tensor"), None),
    P(None, "tensor"),
    P(None, "tensor"),
)


def solution(mesh):
    return jax.shard_map(body, mesh=mesh, in_specs=IN_SPECS, out_specs=OUT_SPECS, check_vma=False)
```

time: 619 us -> 352 us (0.57); the launches traced: 610 us -> 352 us
  matrix products: 167 us -> 2.21 us
  Pallas kernels: 0 us -> 93.3 us
  local copies, waits for them, and re-layouts: 82.3 us -> 9.36 us
  waiting for transfers between devices: 244 us -> 176 us
  other arithmetic: 36 us -> 1.46 us
  blocking collectives: 64.1 us -> 54.1 us
    dot_general x15 -> x0, matrix products: 103 us -> none  [the longest x8 66.8 us: mm_nt(): lax.dot_general(left, right, (((1,), (1,)), ((), ())), preferred_element_...]
    pallas_call x0 -> x1, Pallas kernels: none -> 93.3 us  [run_layer(): pl.pallas_call(kernel, out_shape=(shape((rows, width), NARROW), shape((ro...]
    all_gather x6 -> x3, waiting for transfers between devices: 241 us -> 175 us  [spread(): lax.all_gather(block, everyone, axis=0, tiled=True)]
    dot_general x9 -> x2, matrix products: 49.7 us -> 2.21 us  [mm(): return jnp.dot(left, right, preferred_element_type=WIDE)]
    convert_element_type x2 -> x0, other arithmetic: 27.4 us -> none  [the longest x1 17.1 us: body(): grad_scores = (probs_wide * (grad_probs - inside)).astype(NARROW)]
    reshape x8 -> x6, local copies, waits for them, and re-layouts: 25.1 us -> 1.78 us  [the longest x1 1.3 us: body(): lax.dynamic_slice_in_dim(sentence_row_mask, place * rows, rows)]
    unnamed x99 -> x26, local copies, waits for them, and re-layouts: 22.7 us -> 3.61 us
    convert_element_type x8 -> x0, local copies, waits for them, and re-layouts: 16.7 us -> none  [the longest x3 6.36 us: body(): item.astype(NARROW).reshape(rows, width)]
  transfers between devices with their start and end apart: 6 -> 3, of which waited for: 6 -> 3; matrix products, arithmetic and copies ran while one was open for 15% -> 2% of each run, Pallas kernels for 0% -> 0%
where the time goes in v2:
time: 352 us
  waiting for transfers between devices  176 us (50%)
  Pallas kernels  93.3 us (27%)
  blocking collectives  54.1 us (15%)
  between operations  14.7 us (4%)
  local copies, waits for them, and re-layouts  9.36 us (3%)
    all_gather x3, waiting for transfers between devices, spread(): lax.all_gather(block, everyone, axis=0, tiled=True)  175 us
    pallas_call x1, Pallas kernels, run_layer(): pl.pallas_call(kernel, out_shape=(shape((rows, width), NARROW), shape((ro...  93.3 us
    psum x1, blocking collectives, body(): grads = from_pairs(lax.psum(grads, everyone), groups)  40 us
    unnamed x1, blocking collectives  8.47 us
  transfers between devices with their start and end apart: 3, of which 3 were waited for; matrix products, arithmetic and copies ran while one was open for 2% of the time, Pallas kernels for 0%

profile of v2, /device:TPU:0, one launch (start us, length us, event | category | flops | bytes accessed | tf_op | source)
XLA Modules:
  0.0 351.7 jit_solution(16091379941946482858)
XLA Ops:
  7.2 0.0 copy-start
  7.2 0.0 copy-start.1
  7.2 0.0 copy-start.2
  7.2 0.0 copy-start.3
  7.2 0.0 copy-start.4
  7.2 0.0 copy-start.5
  7.2 0.0 copy-start.6
  7.2 0.0 copy-start.7
  7.3 0.0 copy-start.8
  7.3 0.0 copy-start.9
  7.3 0.0 all-gather.5.cloned.1.call-start
  7.3 0.5 copy-done
  7.9 1.1 fusion.3
  9.0 1.1 fusion.4
  10.1 0.9 copy.33
  11.0 0.7 slice.49
  11.8 0.7 slice.52
  12.5 0.8 concatenate.18
  13.3 0.0 all-gather.5.cloned.1.call-update
  13.3 0.0 all-gather.7.cloned.1.call-start
  13.4 0.7 all-gather.7.cloned.1.call-update
  14.1 0.0 all-gather.9.cloned.1.call-start
  14.1 0.7 all-gather.9.cloned.1.call-update
  14.8 1.2 dynamic-slice
  16.7 0.9 dynamic-update-slice.1
  17.6 0.8 multiply_dynamic-update-slice_fusion
  18.4 8.5 %all-reduce.2 = (f32[768]{0:T(1024)S(1)}, f32[768]{0:T(1024)S(1)}) all-reduce(f32[768]{0:T(1024)S(1)} %multiply_dynamic-update-slice_fusion, f32[768]{0:T(1024)S(1)} %dynamic-update-slice.1), channel_id=1, replica_groups=mesh['dp'=8,'tensor'=4] {'tensor'}, use_global_device_ids=true, to_apply=%add | all-reduce | flops 1536 | bytes 12288
  26.9 0.1 reshape_broadcast_in_dim.6
  26.9 0.1 reshape_broadcast_in_dim.7
  27.0 0.1 reshape_squeeze.6
  27.1 0.1 reshape.41
  27.2 0.1 reshape_squeeze.7
  27.3 0.1 reshape.42
  27.4 0.0 copy-done.3
  27.4 0.0 copy-done.4
  27.4 0.0 copy-done.5
  27.4 0.0 copy-done.6
  27.4 0.0 copy-done.7
  27.5 0.0 copy-done.8
  27.5 0.0 copy-done.9
  27.5 0.6 concatenate.21.vec_ref
  28.2 5.6 %all-gather = f32[4,1,768]{2,1,0:T(1,128)} all-gather(f32[1,1,768]{2,1,0:T(1,128)S(1)} %reshape.54), channel_id=1, replica_groups=mesh['dp'=8,'tensor'=4] {'tensor'}, dimensions={0}, use_global_device_ids=true | all-gather | bytes 15360 | tf_op jit(solution)/shard_map/all_gather | solution.py:397
  33.8 1.3 dynamic-slice_bitcast_fusion
  35.1 0.0 copy-done.1
  35.1 0.0 copy-done.2
  35.1 0.6 maximum_bitcast_fusion.down_t_ref
  35.7 44.2 %all-gather.5.cloned.1.call-done = bf16[3072,768]{1,0:T(8,128)(2,1)} async-done(((bf16[96,768]{1,0:T(8,128)(2,1)}), bf16[3072,768]{1,0:T(8,128)(2,1)}) %all-gather.5.cloned.1.call-update) | async-done | bytes 4718608 | tf_op jit(solution)/shard_map/all_gather | solution.py:392
  79.8 65.4 %all-gather.7.cloned.1.call-done = bf16[3072,768]{1,0:T(8,128)(2,1)} async-done(((bf16[96,768]{1,0:T(8,128)(2,1)}), bf16[3072,768]{1,0:T(8,128)(2,1)}) %all-gather.7.cloned.1.call-update) | async-done | bytes 4718608 | tf_op jit(solution)/shard_map/all_gather | solution.py:392
  145.3 65.4 %all-gather.9.cloned.1.call-done = bf16[3072,768]{1,0:T(8,128)(2,1)} async-done(((bf16[96,768]{1,0:T(8,128)(2,1)}), bf16[3072,768]{1,0:T(8,128)(2,1)}) %all-gather.9.cloned.1.call-update) | async-done | bytes 4718608 | tf_op jit(solution)/shard_map/all_gather | solution.py:392
  210.7 93.3 %shard_map.246 = (bf16[1024,768]{1,0:T(8,128)(2,1)}, bf16[1024,768]{1,0:T(8,128)(2,1)}, f32[16,768]{1,0:T(8,128)}) custom-call(bf16[1024,768]{1,0:T(8,128)(2,1)} %x_ref.1, bf16[1024,768]{1,0:T(8,128)(2,1)} %gout_ref.1, bf16[4,768,768]{2,1,0:T(8,128)(2,1)} %bitcast.16, bf16[4,768,768]{2,1,0:T(8,128)(2,1)} %bitcast.17, bf16[4,768,768]{2,1,0:T(8,128)(2,1)} %bitcast.18, ...), custom_call_target="tpu_custom_call" | custom-call | tf_op jit(solution)/shard_map/pallas_call | solution.py:303
  304.0 40.0 %psum.7 = f32[16,768]{1,0:T(8,128)S(1)} all-reduce(f32[16,768]{1,0:T(8,128)} %get-tuple-element.9), channel_id=1, replica_groups=mesh['dp'=8,'tensor'=4] {'tensor','dp'}, use_global_device_ids=true, to_apply=%region_0.0 | all-reduce | flops 12288 | bytes 98304 | tf_op jit(solution)/shard_map/psum | solution.py:417
  344.1 0.1 reshape.45
  344.2 0.1 reshape.46
  344.3 0.1 pad_maximum_fusion
  344.3 0.1 reshape.47
  344.5 0.7 fusion.9
  (22 shorter events, 0.1 us)
Async XLA Ops:
  7.2 0.7 copy-start
  7.2 27.9 %copy-start.1 = (bf16[768,8]{0,1:T(8,128)(2,1)S(1)}, bf16[768,8]{0,1:T(8,128)(2,1)}, u32[]{:S(2)}) copy-start(bf16[768,8]{0,1:T(8,128)(2,1)} %param.36) | copy-start | bytes 36868
  7.2 27.9 %copy-start.2 = (bf16[768,8]{0,1:T(8,128)(2,1)S(1)}, bf16[768,8]{0,1:T(8,128)(2,1)}, u32[]{:S(2)}) copy-start(bf16[768,8]{0,1:T(8,128)(2,1)} %param.37) | copy-start | bytes 36868
  7.2 20.2 %copy-start.3 = (f32[768]{0:T(1024)S(1)}, f32[768]{0:T(1024)}, u32[]{:S(2)}) copy-start(f32[768]{0:T(1024)} %param.33) | copy-start | bytes 9220
  7.2 20.2 %copy-start.4 = (f32[768]{0:T(1024)S(1)}, f32[768]{0:T(1024)}, u32[]{:S(2)}) copy-start(f32[768]{0:T(1024)} %param.35) | copy-start | bytes 9220
  7.2 20.2 %copy-start.5 = (f32[768]{0:T(1024)S(1)}, f32[768]{0:T(1024)}, u32[]{:S(2)}) copy-start(f32[768]{0:T(1024)} %param.40) | copy-start | bytes 9220
  7.2 20.2 %copy-start.6 = (f32[768]{0:T(1024)S(1)}, f32[768]{0:T(1024)}, u32[]{:S(2)}) copy-start(f32[768]{0:T(1024)} %param.41) | copy-start | bytes 9220
  7.2 20.2 %copy-start.7 = (f32[768]{0:T(1024)S(1)}, f32[768]{0:T(1024)}, u32[]{:S(2)}) copy-start(f32[768]{0:T(1024)} %param.42) | copy-start | bytes 9220
  7.3 20.2 %copy-start.8 = (f32[768]{0:T(1024)S(1)}, f32[768]{0:T(1024)}, u32[]{:S(2)}) copy-start(f32[768]{0:T(1024)} %param.43) | copy-start | bytes 9220
  7.3 20.2 %copy-start.9 = (f32[768]{0:T(1024)S(1)}, f32[768]{0:T(1024)}, u32[]{:S(2)}) copy-start(f32[768]{0:T(1024)} %param.34) | copy-start | bytes 9220
  7.3 72.6 %all-gather.5.cloned.1.call-start = ((), (), s32[]{:S(2)}) async-start(), calls=%async_computation | async-start | bytes 4866048 | tf_op jit(solution)/shard_map/all_gather | solution.py:392
  13.3 131.9 %all-gather.7.cloned.1.call-start = ((), (), s32[]{:S(2)}) async-start(), calls=%async_computation.1 | async-start | bytes 4866048 | tf_op jit(solution)/shard_map/all_gather | solution.py:392
  14.1 196.6 %all-gather.9.cloned.1.call-start = ((), (), s32[]{:S(2)}) async-start(), calls=%async_computation.2 | async-start | bytes 4866048 | tf_op jit(solution)/shard_map/all_gather | solution.py:392
Sparse Core Ops, SparseCore 0:
  13.4 66.3 all-gather.4
  82.8 62.4 all-gather.6
  148.2 62.4 all-gather.8

commit v3 on v2

--- a/solution.py
+++ b/solution.py
@@ -22,6 +22,129 @@
 KEY_SPANS = ((0, 128), (128, 384), (128, 512), (256, 512))
 SPAN_STARTS = (0, 128, 384, 768)
 SPAN_TOTAL = 1024
+BY_MESH = pl.DeviceIdType.MESH
+
+ARRIVALS = (
+    ("Z1", "Z2", "Z3", "X0", "X1", "X2", "X3", "Y0", "Y1", "Y2", "Y3")
+    + ("D0a", "D0b", "D1", "D2a", "D2b", "D3", "C")
+    + tuple("C" + kind + str(k) for kind in "ZXYD" for k in range(4) if kind + str(k) != "Z0")
+)
+SIGNALS = {name: i for i, name in enumerate(ARRIVALS + ("Z2down",))}
+PASS_ON = {
+    "own": (("X0", "x", ""), ("Y0", "y", ""), ("Z1", "up", ""), ("Z3", "down", ""), ("C", "core", "")),
+    "X0": (("X1", "up", ""), ("D0b", "y", "b"), ("CX0", "core", "")),
+    "Y0": (("Y3", "down", ""), ("D0a", "x", "a"), ("CY0", "core", "")),
+    "Z1": (("Y1", "y", ""), ("CZ1", "core", "")),
+    "Z3": (("X3", "x", ""), ("CZ3", "core", "")),
+    "X1": (("CX1", "core", ""),),
+    "Y3": (("CY3", "core", ""),),
+    "Z2": (("X2", "x", ""), ("Y2", "y", ""), ("CZ2", "core", "")),
+    "Y1": (("D1", "x", ""), ("CY1", "core", "")),
+    "X3": (("D3", "y", ""), ("CX3", "core", "")),
+    "X2": (("D2b", "y", "b"), ("CX2", "core", "")),
+    "Y2": (("D2a", "x", "a"), ("CY2", "core", "")),
+    "D0b": (("CD0", "core", ""),),
+    "D1": (("CD1", "core", ""),),
+    "D2b": (("CD2", "core", ""),),
+    "D3": (("CD3", "core", ""),),
+}
+ROUNDS = (
+    ("own",),
+    ("X0", "Y0", "Z1", "Z3"),
+    ("X1", "Y3", "Z2", "Y1", "X3"),
+    ("X2", "Y2", "D0a", "D0b", "D1", "D3"),
+    ("D2a", "D2b"),
+    tuple(name for name in ARRIVALS if name[0] == "C"),
+)
+
+
+def in_rounds(*rounds):
+    return [(group, name) for number, group in rounds for name in ROUNDS[number]]
+
+
+PLAN = {
+    "start": {0: in_rounds((0, 1), (0, 2))},
+    "masked": {0: in_rounds(*((number, group) for number in range(1, 6) for group in range(3)))},
+}
+
+
+class Gather:
+    def __init__(self, blocks, send, recv):
+        self.blocks, self.send, self.recv = blocks, send, recv
+        self.d, self.t = lax.axis_index("dp"), lax.axis_index("tensor")
+        self.depth = blocks[0].shape[1] // 8
+        self.z, self.y = self.d // 2, lax.rem(self.d, 2)
+        self.tx = lax.rem(self.t + 2, 4)
+        self.tc = self.t + 1 - 2 * lax.rem(self.t, 2)
+        self.txc = lax.rem(self.tc + 2, 4)
+        self.middle = (self.z == 1) | (self.z == 2)
+
+    def peer(self, kind):
+        return {
+            "x": (self.d, self.tx),
+            "y": (self.z * 2 + 1 - self.y, self.t),
+            "core": (self.d, self.tc),
+            "up": (lax.rem(self.z + 1, 4) * 2 + self.y, self.t),
+            "down": (lax.rem(self.z + 3, 4) * 2 + self.y, self.t),
+        }[kind]
+
+    def part(self, group, name, half=""):
+        if name == "own":
+            dp, t = self.d, self.t
+        elif name == "C":
+            dp, t = self.d, self.tc
+        else:
+            kind = name[-2] if name[-1].isdigit() else name[-3]
+            k = int(name[-1] if name[-1].isdigit() else name[-2])
+            half = half or (name[-1] if not name[-1].isdigit() else "")
+            near, far = (self.tc, self.txc) if name[0] == "C" else (self.t, self.tx)
+            dp = lax.rem(self.z - k + 4, 4) * 2 + (self.y if kind in "ZX" else 1 - self.y)
+            t = near if kind in "ZY" else far
+        size = self.depth // 2 if half else self.depth
+        first = dp * self.depth + (size if half == "b" else 0)
+        return self.blocks[group].at[t, pl.ds(pl.multiple_of(first, 16), size), :]
+
+    def copy(self, group, part, name, to, sender=None):
+        return pltpu.make_async_remote_copy(
+            src_ref=part,
+            dst_ref=part,
+            send_sem=self.send.at[group, SIGNALS[sender or name]],
+            recv_sem=self.recv.at[group, SIGNALS[name]],
+            device_id=self.peer(to),
+            device_id_type=BY_MESH,
+        )
+
+    def outgoing(self, group, name):
+        whole = name[:2] if name[0] == "D" else name
+        return [
+            self.copy(group, self.part(group, whole, half), out, to)
+            for out, to, half in PASS_ON.get(name, ())
+        ]
+
+    def relayed(self, group, name):
+        to, sender = ("up", "Z2") if name == "Z1" else ("down", "Z2down")
+        return self.copy(group, self.part(group, name), "Z2", to, sender)
+
+    def step(self, group, name):
+        if name != "own":
+            self.copy(group, self.part(group, name), name, "x").wait_recv()
+        for copy in self.outgoing(group, name):
+            copy.start()
+        if name in ("Z1", "Z3"):
+
+            @pl.when(self.middle)
+            def _():
+                self.relayed(group, name).start()
+
+    def finish(self, group):
+        for name in PASS_ON:
+            for copy in self.outgoing(group, name):
+                copy.wait_send()
+
+        @pl.when(self.middle)
+        def _():
+            self.relayed(group, "Z1").wait_send()
+            self.relayed(group, "Z3").wait_send()
 
 
 def mm(left, right):
@@ -58,41 +181,117 @@
     return jnp.where(lane < HEAD_DIM, low, pltpu.roll(high, HEAD_DIM, 1))
 
 
-def kernel(
-    x_ref,
-    gout_ref,
-    a_ref,
-    b_ref,
-    c_ref,
-    vec_ref,
-    upb_ref,
-    down_t_ref,
-    seg_ref,
-    live_ref,
-    out_ref,
-    gin_ref,
-    gl_ref,
-    wq,
-    wk,
-    wv,
-    wo,
-    q,
-    k,
-    v,
-    probs,
-    ctx,
-    n1,
-    s1,
-    act,
-    slope,
-    acc,
-    mask,
-    u_t,
-):
+def kernel(plan, *refs):
+    if plan is not None:
+        (x_ref, gout_ref, wq_ref, wk_ref, wv_ref, wo_ref, up_ref, down_ref, dq_ref, dv_ref, uq_ref, uv_ref) = refs[:12]
+        (bq_ref, bv_ref, bup_ref, vec_ref, down_t_ref, seg_ref, live_ref) = refs[12:19]
+        (out_ref, gin_ref, glq_ref, glv_ref) = refs[19:23]
+        (wq, wk, wv, wo, q, k, v, probs, ctx, n1, s1, act, slope, acc, mask, u_t) = refs[23:39]
+        (a_ref, b_ref, c_ref, bias, biases, part, near, far) = refs[39:47]
+        (send, recv, bias_send, bias_recv, near_send, near_recv, far_send, far_recv) = refs[47:]
+    else:
+        (x_ref, gout_ref, a_ref, b_ref, c_ref, biases_ref, vec_ref, down_t_ref, seg_ref, live_ref) = refs[:10]
+        (out_ref, gin_ref, gl_ref) = refs[10:13]
+        (wq, wk, wv, wo, q, k, v, probs, ctx, n1, s1, act, slope, acc, mask, u_t, biases) = refs[13:]
     rows, width = x_ref.shape
     seqs = rows // SEQ
     pairs = width // LANES
     groups = a_ref.shape[0]
+
+    if plan is not None:
+        gather = Gather((a_ref, b_ref, c_ref), send, recv)
+        me_d, me_t = gather.d, gather.t
+        dps = width // wq_ref.shape[0]
+        depth = wq_ref.shape[0]
+        others_t = [lax.rem(me_t + i, groups) for i in range(1, groups)]
+        others_d = [lax.rem(me_d + i, dps) for i in range(1, dps)]
+        seg_rows = pl.ds(pl.multiple_of(me_t * (rows // LANES), rows // LANES), rows // LANES)
+        barrier = pltpu.get_barrier_semaphore()
+        for other in others_t:
+            pl.semaphore_signal(barrier, inc=1, device_id=(me_d, other), device_id_type=BY_MESH)
+        for other in others_d:
+            pl.semaphore_signal(barrier, inc=1, device_id=(other, me_t), device_id_type=BY_MESH)
+
+        mine = pl.ds(pl.multiple_of(me_d * depth, depth), depth)
+        query = wq_ref[...].astype(WIDE) + ADAPTER_SCALE * mm(dq_ref[mine, :], uq_ref[...])
+        query = query * SCORE_SCALE
+        value = wv_ref[...].astype(WIDE) + ADAPTER_SCALE * mm(dv_ref[mine, :], uv_ref[...])
+        key = wk_ref[...].astype(WIDE)
+        out_t = jnp.transpose(wo_ref[...].astype(WIDE))
+        a_ref[me_t, mine, 0:128] = query[:, 0:128].astype(NARROW)
+        a_ref[me_t, mine, 128:256] = key[:, 0:128].astype(NARROW)
+        a_ref[me_t, mine, 256:384] = value[:, 0:128].astype(NARROW)
+        a_ref[me_t, mine, 384:512] = jnp.concatenate([query[:, 128:], key[:, 128:]], axis=1).astype(NARROW)
+        a_ref[me_t, mine, 512:640] = jnp.concatenate([value[:, 128:], out_t[:, 128:]], axis=1).astype(NARROW)
+        a_ref[me_t, mine, 640:768] = out_t[:, 0:128].astype(NARROW)
+        bias[me_t, 0:1, :] = bup_ref[...]
+        bias[me_t, 1:2, 0:192] = bq_ref[...] * SCORE_SCALE
+        bias[me_t, 1:2, 256:448] = bv_ref[...]
+        pl.semaphore_wait(barrier, len(others_t) + len(others_d))
+
+        def bias_copy(i):
+            return pltpu.make_async_remote_copy(
+                src_ref=bias.at[me_t],
+                dst_ref=bias.at[me_t],
+                send_sem=bias_send.at[i],
+                recv_sem=bias_recv.at[i],
+                device_id=(me_d, others_t[i]),
+                device_id_type=BY_MESH,
+            )
+
+        for name in ("own",):
+            gather.step(0, name)
+        b_ref[me_t, mine, :] = up_ref[...]
+        c_ref[me_t, mine, :] = jnp.transpose(down_ref[...].astype(WIDE)).astype(NARROW)
+        for i in range(len(others_t)):
+            bias_copy(i).start()
+    else:
+        seg_rows = pl.ds(0, rows // LANES)
+        biases[...] = biases_ref[...]
+
+    def ticks(place, step=None):
+        if plan is None:
+            return
+        for at, names in plan.get(place, {}).items():
+            if step is None:
+                for group, name in names:
+                    gather.step(group, name)
+            else:
+
+                @pl.when(step == at)
+                def _():
+                    for group, name in names:
+                        gather.step(group, name)
+
+    segment_ids = seg_ref[seg_rows, :]
+    live_flags = live_ref[seg_rows, :]
+    ticks("start")
+    place = lax.broadcasted_iota(jnp.int32, (LANES, LANES), 0) == lax.broadcasted_iota(
+        jnp.int32, (LANES, LANES), 1
+    )
+    for seq in range(seqs):
+        wide_ids = []
+        key_ids = []
+        for block in range(4):
+            row = seq * 4 + block
+            ids = segment_ids[row : row + 1, :].astype(WIDE)
+            live = live_flags[row : row + 1, :]
+            key = jnp.where(live == 1, ids, -1.0)
+            wide_ids.append(ids)
+            key_ids.append(jnp.transpose(jnp.broadcast_to(key, (LANES, LANES))))
+        for block in range(1, 4):
+            start, stop = KEY_SPANS[block]
+            for j in range((stop - start) // LANES):
+                kb = start // LANES + j
+                seen = key_ids[kb] == wide_ids[block]
+                if kb == block:
+                    seen = seen | place
+                at = SPAN_STARTS[block] + j * LANES
+                mask[seq, at : at + LANES, :] = jnp.where(seen, 0.0, NEG_FILL)
+
+    u_t[...] = mm_nt(down_t_ref[...], x_ref[...]).astype(NARROW)
+
+    ticks("masked")
 
     for group in range(groups):
         at = slice(group * LANES, (group + 1) * LANES)
@@ -111,37 +310,34 @@
         wv[:, at] = pair_select(first, second).astype(NARROW)
         wo[:, at] = pair_select(pltpu.roll(first, HEAD_DIM, 1), pltpu.roll(second, HEAD_DIM, 1)).astype(NARROW)
 
-    place = lax.broadcasted_iota(jnp.int32, (LANES, LANES), 0) == lax.broadcasted_iota(
-        jnp.int32, (LANES, LANES), 1
-    )
-    for seq in range(seqs):
-        wide_ids = []
-        key_ids = []
-        for block in range(4):
-            row = seq * 4 + block
-            ids = seg_ref[row : row + 1, :].astype(WIDE)
-            live = live_ref[row : row + 1, :]
-            key = jnp.where(live == 1, ids, -1.0)
-            wide_ids.append(ids)
-            key_ids.append(jnp.transpose(jnp.broadcast_to(key, (LANES, LANES))))
-        for block in range(1, 4):
-            start, stop = KEY_SPANS[block]
-            for j in range((stop - start) // LANES):
-                kb = start // LANES + j
-                seen = key_ids[kb] == wide_ids[block]
-                if kb == block:
-                    seen = seen | place
-                at = SPAN_STARTS[block] + j * LANES
-                mask[seq, at : at + LANES, :] = jnp.where(seen, 0.0, NEG_FILL)
-
-    u_t[...] = mm_nt(down_t_ref[...], x_ref[...]).astype(NARROW)
+    if plan is not None:
+        for i in range(len(others_t)):
+            pltpu.make_async_remote_copy(
+                src_ref=bias.at[me_t],
+                dst_ref=bias.at[lax.rem(me_t + groups - 1 - i, groups)],
+                send_sem=bias_send.at[i],
+                recv_sem=bias_recv.at[i],
+                device_id=(me_d, others_t[i]),
+                device_id_type=BY_MESH,
+            ).wait_recv()
+        for group in range(groups):
+            biases[2 + group : 3 + group, :] = bias[group, 0:1, :]
+            biases[0:1, group * LANES : (group + 1) * LANES] = bias[group, 1:2, 0:128]
+            biases[1:2, group * LANES : (group + 1) * LANES] = bias[group, 1:2, 256:384]
+        for half in range(groups // 2):
+            at = slice((groups + half) * LANES, (groups + half + 1) * LANES)
+            for row, first in ((0, 128), (1, 384)):
+                low = jnp.broadcast_to(bias[2 * half, 1:2, first : first + 128], (8, LANES))
+                high = jnp.broadcast_to(bias[2 * half + 1, 1:2, first : first + 128], (8, LANES))
+                biases[row : row + 1, at] = pair_select(low, high)[0:1]
 
     def project(step, carry):
+        ticks("project", step)
         at = pl.ds(pl.multiple_of(step * 256, 256), 256)
         xs = x_ref[...]
-        q[:, at] = (mm(xs, wq[:, at]) + vec_ref[0:1, at]).astype(NARROW)
+        q[:, at] = (mm(xs, wq[:, at]) + biases[0:1, at]).astype(NARROW)
         k[:, at] = mm(xs, wk[:, at]).astype(NARROW)
-        v[:, at] = (mm(xs, wv[:, at]) + vec_ref[1:2, at]).astype(NARROW)
+        v[:, at] = (mm(xs, wv[:, at]) + biases[1:2, at]).astype(NARROW)
         return carry
 
     lax.fori_loop(0, width // 256, project, 0)
@@ -159,6 +355,7 @@
         return jnp.transpose(own)
 
     def attend(step, carry):
+        ticks("attend", step)
         seq = step // pairs
         pair = step - seq * pairs
         at = pl.ds(pl.multiple_of(pair * LANES, LANES), LANES)
@@ -184,40 +381,44 @@
     lax.fori_loop(0, seqs * pairs, attend, 0)
 
     def first_norm(step, carry):
+        ticks("first_norm", step)
         at = pl.ds(pl.multiple_of(step * 256, 256), 256)
-        r = x_ref[at, :].astype(WIDE) + (mm_nt(ctx[at, :], wo[...]) + vec_ref[2:3, :])
+        r = x_ref[at, :].astype(WIDE) + (mm_nt(ctx[at, :], wo[...]) + vec_ref[0:1, :])
         centered = r - row_mean(r)
         inverse = lax.rsqrt(row_mean(centered * centered) + EPSILON)
         normed = centered * inverse
         n1[at, :] = normed
         s1[at, :] = inverse
-        out_ref[at, :] = (normed * vec_ref[4:5, :] + vec_ref[5:6, :]).astype(NARROW)
+        out_ref[at, :] = (normed * vec_ref[2:3, :] + vec_ref[3:4, :]).astype(NARROW)
         return carry
 
     lax.fori_loop(0, rows // 256, first_norm, 0)
 
     def up(group, carry):
+        ticks("up", group)
         for j in range(width // 256):
             cols = slice(j * 256, (j + 1) * 256)
             at = pl.ds(pl.multiple_of(group * width + j * 256, 256), 256)
-            inner = mm(out_ref[...], b_ref[group, :, cols]) + upb_ref[0:1, at]
+            inner = mm(out_ref[...], b_ref[group, :, cols]) + biases[pl.ds(2 + group, 1), cols]
             value, grad = gelu_parts(inner)
             act[:, at] = value.astype(NARROW)
             slope[:, at] = grad.astype(NARROW)
         return carry
 
+    ticks("before up")
     lax.fori_loop(0, groups, up, 0)
+    ticks("before down")
 
     def second_norm(step, carry):
         at = pl.ds(pl.multiple_of(step * 256, 256), 256)
-        r = n1[at, :] * vec_ref[4:5, :] + vec_ref[5:6, :] + vec_ref[3:4, :]
+        r = n1[at, :] * vec_ref[2:3, :] + vec_ref[3:4, :] + vec_ref[1:2, :]
         for group in range(groups):
             r = r + mm_nt(act[at, group * width : (group + 1) * width], c_ref[group])
         centered = r - row_mean(r)
         inverse = lax.rsqrt(row_mean(centered * centered) + EPSILON)
         normed = centered * inverse
-        out_ref[at, :] = (normed * vec_ref[6:7, :] + vec_ref[7:8, :]).astype(NARROW)
-        e = gout_ref[at, :].astype(WIDE) * vec_ref[6:7, :]
+        out_ref[at, :] = (normed * vec_ref[4:5, :] + vec_ref[5:6, :]).astype(NARROW)
+        e = gout_ref[at, :].astype(WIDE) * vec_ref[4:5, :]
         acc[at, :] = inverse * (e - row_mean(e) - normed * row_mean(e * normed))
         return carry
 
@@ -233,7 +434,7 @@
             grad = (mm(low, c_ref[group]) * slope[at, cols].astype(WIDE)).astype(NARROW)
             total = total + mm_nt(grad, b_ref[group])
         normed = n1[at, :]
-        e = total * vec_ref[4:5, :]
+        e = total * vec_ref[2:3, :]
         first = s1[at, :] * (e - row_mean(e) - normed * row_mean(e * normed))
         acc[at, :] = first
         ctx[at, :] = mm(first.astype(NARROW), wo[...]).astype(NARROW)
@@ -278,6 +479,9 @@
 
     lax.fori_loop(0, seqs * pairs, attend_back, 0)
 
+    grad_q = mm(u_t[0:8, :], q[...]) * (ADAPTER_SCALE * SCORE_SCALE)
+    grad_v = mm(u_t[8:16, :], v[...]) * ADAPTER_SCALE
+
     def input_back(step, carry):
         at = pl.ds(pl.multiple_of(step * 256, 256), 256)
         total = acc[at, :] + mm_nt(q[at, :], wq[...])
@@ -286,22 +490,99 @@
         gin_ref[at, :] = total.astype(NARROW)
         return carry
 
-    lax.fori_loop(0, rows // 256, input_back, 0)
-
-    gl_ref[0:8, :] = mm(u_t[0:8, :], q[...]) * (ADAPTER_SCALE * SCORE_SCALE)
-    gl_ref[8:16, :] = mm(u_t[8:16, :], v[...]) * ADAPTER_SCALE
-
-
-def run_layer(x, gout, a, b, c, vectors, up_bias, down_t, seg, live):
-    rows, width = x.shape
-    hidden = up_bias.shape[1]
+    if plan is None:
+        gl_ref[0:8, :] = grad_q
+        gl_ref[8:16, :] = grad_v
+        lax.fori_loop(0, rows // 256, input_back, 0)
+        return
+
+    for group in range(groups):
+        for row, grad in ((0, grad_q), (8, grad_v)):
+            part[group, row : row + 8, 0:128] = grad[:, group * LANES : (group + 1) * LANES]
+            other = groups + group // 2
+            part[group, row : row + 8, 128:256] = grad[:, other * LANES : (other + 1) * LANES]
+
+    def near_copy(i, slot):
+        return pltpu.make_async_remote_copy(
+            src_ref=part.at[others_t[i]],
+            dst_ref=near.at[slot],
+            send_sem=near_send.at[i],
+            recv_sem=near_recv.at[i],
+            device_id=(me_d, others_t[i]),
+            device_id_type=BY_MESH,
+        )
+
+    def far_copy(i, slot):
+        return pltpu.make_async_remote_copy(
+            src_ref=far.at[me_d],
+            dst_ref=far.at[slot],
+            send_sem=far_send.at[i],
+            recv_sem=far_recv.at[i],
+            device_id=(others_d[i], me_t),
+            device_id_type=BY_MESH,
+        )
+
+    for i in range(len(others_t)):
+        near_copy(i, i).start()
+    lax.fori_loop(0, rows // 512, input_back, 0)
+    total = part[me_t]
+    for i in range(len(others_t)):
+        near_copy(i, i).wait_recv()
+        total = total + near[i]
+    far[me_d] = total
+    for i in range(len(others_d)):
+        far_copy(i, me_d).start()
+    lax.fori_loop(rows // 512, rows // 256, input_back, 0)
+    for group in range(3):
+        gather.finish(group)
+    for i in range(len(others_t)):
+        bias_copy(i).wait_send()
+        near_copy(i, i).wait_send()
+    for i in range(len(others_d)):
+        far_copy(i, lax.rem(me_d + dps - 1 - i, dps)).wait_recv()
+    total = far[0]
+    for i in range(1, dps):
+        total = total + far[i]
+    last = jnp.where(lax.rem(me_t, 2) == 0, total[:, 128:], pltpu.roll(total[:, 128:], HEAD_DIM, 1))
+    glq_ref[:, 0:128] = total[0:8, 0:128]
+    glv_ref[:, 0:128] = total[8:16, 0:128]
+    glq_ref[:, 128:192] = last[0:8, 0:HEAD_DIM]
+    glv_ref[:, 128:192] = last[8:16, 0:HEAD_DIM]
+    for i in range(len(others_d)):
+        far_copy(i, me_d).wait_send()
+
+
+def scratch(rows, width, hidden):
     pairs = width // LANES
     seqs = rows // SEQ
-    shape = jax.ShapeDtypeStruct
     square = pltpu.VMEM((width, width), NARROW)
     plane = pltpu.VMEM((rows, width), NARROW)
+    return [
+        square,
+        square,
+        square,
+        square,
+        plane,
+        plane,
+        plane,
+        pltpu.VMEM((seqs * pairs, SPAN_TOTAL, 2 * LANES), NARROW),
+        plane,
+        pltpu.VMEM((rows, width), WIDE),
+        pltpu.VMEM((rows, 1), WIDE),
+        pltpu.VMEM((rows, hidden), NARROW),
+        pltpu.VMEM((rows, hidden), NARROW),
+        pltpu.VMEM((rows, width), WIDE),
+        pltpu.VMEM((seqs, SPAN_TOTAL, LANES), WIDE),
+        pltpu.VMEM((2 * ADAPTER_RANK, rows), NARROW),
+    ]
+
+
+def run_layer(x, gout, a, b, c, biases, vectors, down_t, seg, live):
+    rows, width = x.shape
+    shape = jax.ShapeDtypeStruct
+    hidden = b.shape[0] * b.shape[2]
     return pl.pallas_call(
-        kernel,
+        functools.partial(kernel, None),
         out_shape=(
             shape((rows, width), NARROW),
             shape((rows, width), NARROW),
@@ -309,26 +590,52 @@
         ),
         in_specs=[pl.BlockSpec(memory_space=pltpu.VMEM)] * 10,
         out_specs=[pl.BlockSpec(memory_space=pltpu.VMEM)] * 3,
-        scratch_shapes=[
-            square,
-            square,
-            square,
-            square,
-            plane,
-            plane,
-            plane,
-            pltpu.VMEM((seqs * pairs, SPAN_TOTAL, 2 * LANES), NARROW),
-            plane,
-            pltpu.VMEM((rows, width), WIDE),
-            pltpu.VMEM((rows, 1), WIDE),
-            pltpu.VMEM((rows, hidden), NARROW),
-            pltpu.VMEM((rows, hidden), NARROW),
-            pltpu.VMEM((rows, width), WIDE),
-            pltpu.VMEM((seqs, SPAN_TOTAL, LANES), WIDE),
-            pltpu.VMEM((2 * ADAPTER_RANK, rows), NARROW),
+        scratch_shapes=scratch(rows, width, hidden) + [pltpu.VMEM((8, width), WIDE)],
+        compiler_params=pltpu.CompilerParams(vmem_limit_bytes=63 << 20),
+    )(x, gout, a, b, c, biases, vectors, down_t, seg, live)
+
+
+def run_layer_and_gather(x, gout, blocks, adapters, biases, vectors, down_t, seg, live):
+    rows, width = x.shape
+    groups = width // blocks[0].shape[1]
+    dps = width // blocks[0].shape[0]
+    shape = jax.ShapeDtypeStruct
+    gathered = pltpu.VMEM((groups, width, width), NARROW)
+    signals = pltpu.SemaphoreType.DMA
+    operands = (x, gout, *blocks, *adapters, *biases, vectors, down_t, seg, live)
+    return pl.pallas_call(
+        functools.partial(kernel, PLAN),
+        out_shape=(
+            shape((rows, width), NARROW),
+            shape((rows, width), NARROW),
+            shape((ADAPTER_RANK, width // groups), WIDE),
+            shape((ADAPTER_RANK, width // groups), WIDE),
+        ),
+        in_specs=[pl.BlockSpec(memory_space=pltpu.VMEM)] * len(operands),
+        out_specs=[pl.BlockSpec(memory_space=pltpu.VMEM)] * 4,
+        scratch_shapes=scratch(rows, width, groups * width)
+        + [
+            gathered,
+            gathered,
+            gathered,
+            pltpu.VMEM((groups, 8, width), WIDE),
+            pltpu.VMEM((8, width), WIDE),
+            pltpu.VMEM((groups, 2 * ADAPTER_RANK, 2 * LANES), WIDE),
+            pltpu.VMEM((groups - 1, 2 * ADAPTER_RANK, 2 * LANES), WIDE),
+            pltpu.VMEM((dps, 2 * ADAPTER_RANK, 2 * LANES), WIDE),
+            signals((3, len(SIGNALS))),
+            signals((3, len(SIGNALS))),
+            signals((groups - 1,)),
+            signals((groups - 1,)),
+            signals((groups - 1,)),
+            signals((groups - 1,)),
+            signals((dps - 1,)),
+            signals((dps - 1,)),
         ],
-        compiler_params=pltpu.CompilerParams(vmem_limit_bytes=63 << 20),
-    )(x, gout, a, b, c, vectors, up_bias, down_t, seg, live)
+        compiler_params=pltpu.CompilerParams(
+            collective_id=0, has_side_effects=True, vmem_limit_bytes=63 << 20
+        ),
+    )(*operands)
 
 
 def in_pairs(block, groups):
@@ -344,6 +651,7 @@
 
 
 def body(
+    grid,
     layer_input_rows,
     output_gradient,
     query_weight,
@@ -370,8 +678,34 @@
 ):
     everyone = ("tensor", "dp")
     rows, width = layer_input_rows.shape
-    groups = width // query_weight.shape[1]
-    depth = query_weight.shape[0]
+    depth, across = query_weight.shape
+    groups = width // across
+    vectors = jnp.stack(
+        [
+            output_bias_vector,
+            down_bias_vector,
+            first_norm_gain,
+            first_norm_bias,
+            second_norm_gain,
+            second_norm_bias,
+        ]
+    )
+    down_t = jnp.concatenate([query_down_frozen, value_down_frozen], axis=1).T
+    segment_rows = segments.reshape(-1, LANES)
+    live_rows = sentence_row_mask.reshape(-1, LANES)
+    if grid == (8, 4):
+        return run_layer_and_gather(
+            layer_input_rows,
+            output_gradient,
+            (query_weight, key_weight, value_weight, output_weight, up_weight, down_weight),
+            (query_down_frozen, value_down_frozen, query_up_trained, value_up_trained),
+            (query_bias_vector[None], value_bias_vector[None], up_bias_vector[None]),
+            vectors,
+            down_t,
+            segment_rows,
+            live_rows,
+        )
+
     place = lax.axis_index("tensor")
     which = lax.axis_index("dp")
 
@@ -395,28 +729,23 @@
     query_bias = lax.all_gather(query_bias_vector * SCORE_SCALE, "tensor", axis=0, tiled=True)
     value_bias = lax.all_gather(value_bias_vector, "tensor", axis=0, tiled=True)
     up_bias = lax.all_gather(up_bias_vector, "tensor", axis=0, tiled=True)
-    vectors = jnp.concatenate(
+    biases = jnp.concatenate(
         [
             in_pairs(query_bias[None], groups),
             in_pairs(value_bias[None], groups),
-            output_bias_vector[None],
-            down_bias_vector[None],
-            first_norm_gain[None],
-            first_norm_bias[None],
-            second_norm_gain[None],
-            second_norm_bias[None],
+            up_bias.reshape(groups, width),
+            jnp.zeros((6 - groups, width), WIDE),
         ],
         axis=0,
     )
-    down_t = jnp.concatenate([query_down_frozen, value_down_frozen], axis=1).T
-    seg = lax.dynamic_slice_in_dim(segments, place * rows, rows).reshape(-1, LANES)
-    live = lax.dynamic_slice_in_dim(sentence_row_mask, place * rows, rows).reshape(-1, LANES)
+    blocks = rows // LANES
+    seg = lax.dynamic_slice_in_dim(segment_rows, place * blocks, blocks)
+    live = lax.dynamic_slice_in_dim(live_rows, place * blocks, blocks)
     output, grad_input, grads = run_layer(
-        layer_input_rows, output_gradient, a, b, c, vectors, up_bias[None], down_t, seg, live
+        layer_input_rows, output_gradient, a, b, c, biases, vectors, down_t, seg, live
     )
     grads = from_pairs(lax.psum(grads, everyone), groups)
-    mine = query_up_trained.shape[1]
-    grads = lax.dynamic_slice_in_dim(grads, place * mine, mine, axis=1)
+    grads = lax.dynamic_slice_in_dim(grads, place * across, across, axis=1)
     return output, grad_input, grads[:ADAPTER_RANK], grads[ADAPTER_RANK:]
 
 
@@ -454,4 +783,6 @@
 
 
 def solution(mesh):
-    return jax.shard_map(body, mesh=mesh, in_specs=IN_SPECS, out_specs=OUT_SPECS, check_vma=False)
+    grid = (mesh.shape["dp"], mesh.shape["tensor"])
+    layer = functools.partial(body, grid)
+    return jax.shard_map(layer, mesh=mesh, in_specs=IN_SPECS, out_specs=OUT_SPECS, check_vma=False)

time: 352 us -> 182 us (0.52)
  waiting for transfers between devices: 176 us -> 0 us
  Pallas kernels: 93.3 us -> 163 us
  blocking collectives: 54.1 us -> 0 us
  between operations: 14.7 us -> 0.66 us
  local copies, waits for them, and re-layouts: 9.36 us -> 15.9 us
    all_gather x3 -> x0, waiting for transfers between devices: 175 us -> none  [spread(): lax.all_gather(block, everyone, axis=0, tiled=True)]
    pallas_call x1, Pallas kernels: 93.3 us -> 163 us  [run_layer_and_gather(): pl.pallas_call(functools.partial(kernel, PLAN), out_shape=(shape((rows, w...]
    psum x1 -> x0, blocking collectives: 40 us -> none  [body(): grads = from_pairs(lax.psum(grads, everyone), groups)]
    unnamed x1 -> x0, blocking collectives: 8.47 us -> none
    unnamed x26 -> x13, local copies, waits for them, and re-layouts: 3.61 us -> 9.89 us
    all_gather x1 -> x0, blocking collectives: 5.58 us -> none  [body(): up_bias = lax.all_gather(up_bias_vector, 'tensor', axis=0, tiled=True)]
    another operation x4 -> x7, local copies, waits for them, and re-layouts: 0.32 us -> 4.76 us  [body(): jnp.stack([output_bias_vector, down_bias_vector, first_norm_gain, first_n...]
  transfers between devices with their start and end apart: 3 -> 0, of which waited for: 3 -> 0; matrix products, arithmetic and copies ran while one was open for 2% -> 0% of each run, Pallas kernels for 0% -> 0%
where the time goes in v3:
time: 182 us; the launch traced here: 181 us
  Pallas kernels  163 us (90%)
  local copies, waits for them, and re-layouts  15.9 us (9%)
    pallas_call x1, Pallas kernels, run_layer_and_gather(): pl.pallas_call(functools.partial(kernel, PLAN), out_shape=(shape((rows, w...  163 us
    unnamed x13, local copies, waits for them, and re-layouts  9.89 us
    another operation x7, local copies, waits for them, and re-layouts, body(): jnp.stack([output_bias_vector, down_bias_vector, first_norm_gain, first_n...  4.76 us

profile of v3, /device:TPU:0, one launch (start us, length us, event | category | flops | bytes accessed | tf_op | source)
XLA Modules:
  0.0 181.2 jit_solution(5314643259884412622)
XLA Ops:
  0.6 0.7 stack.21
  1.3 1.3 broadcast_in_dim.11.refs_14_
  2.6 0.7 stack.22
  3.3 0.7 stack.23
  4.0 0.7 stack.24
  4.7 0.7 stack.25
  5.3 0.7 stack.26
  6.0 0.6 stack.27.refs_15_
  6.7 1.3 maximum_bitcast_fusion.refs_16_
  8.0 1.7 copy.27.refs_7_
  9.7 1.5 copy.28.refs_8_
  11.2 1.5 copy.29.refs_9_
  12.8 163.3 %shard_map.246 = (bf16[1024,768]{1,0:T(8,128)(2,1)}, bf16[1024,768]{1,0:T(8,128)(2,1)}, f32[8,192]{1,0:T(8,128)}, f32[8,192]{1,0:T(8,128)}) custom-call(bf16[1024,768]{1,0:T(8,128)(2,1)} %refs_0_.1, bf16[1024,768]{1,0:T(8,128)(2,1)} %refs_1_.1, bf16[96,192]{1,0:T(8,128)(2,1)} %refs_2_.1, bf16[96,192]{1,0:T(8,128)(2,1)} %refs_3_.1, bf16[96,192]{1,0:T(8,128)(2,1)} %refs_4_.1, ...), custom_call_target="tpu_custom_call" | custom-call | tf_op jit(solution)/shard_map/pallas_call | solution.py:606
  176.1 0.0 copy-start
  176.1 2.8 %copy.34 = bf16[1024,768]{1,0:T(8,128)(2,1)} copy(bf16[1024,768]{1,0:T(8,128)(2,1)} %get-tuple-element.8) | data formatting | bytes 3145728
  178.9 0.0 copy-done
  178.9 0.0 copy-start.2
  178.9 0.0 copy-start.1
  178.9 1.1 copy.35
  180.0 0.0 copy-done.2
  180.0 0.6 copy.36
  180.6 0.0 copy-done.1
  180.6 0.6 copy.37
Async XLA Ops:
  176.1 2.8 %copy-start = (bf16[1024,768]{1,0:T(8,128)(2,1)S(1)}, bf16[1024,768]{1,0:T(8,128)(2,1)}, u32[]{:S(2)}) copy-start(bf16[1024,768]{1,0:T(8,128)(2,1)} %get-tuple-element.9) | copy-start | bytes 4718596
  178.9 1.1 copy-start.2
  178.9 1.7 copy-start.1

commit v4 on v3

--- a/solution.py
+++ b/solution.py
@@ -63,8 +63,11 @@
 
 
 PLAN = {
-    "start": {0: in_rounds((0, 1), (0, 2))},
-    "masked": {0: in_rounds(*((number, group) for number in range(1, 6) for group in range(3)))},
+    "start": {0: in_rounds((1, 0), (0, 1), (2, 0), (1, 1), (3, 0), (0, 2), (4, 0), (5, 0))},
+    "project": {0: in_rounds((2, 1)), 1: in_rounds((1, 2)), 2: in_rounds((3, 1))},
+    "attend": {0: in_rounds((2, 2)), 1: in_rounds((4, 1), (3, 2)), 2: in_rounds((4, 2))},
+    "before up": {0: in_rounds((5, 1))},
+    "before down": {0: in_rounds((5, 2))},
 }
 
 
@@ -155,25 +158,18 @@
     return lax.dot_general(left, right, (((1,), (1,)), ((), ())), preferred_element_type=WIDE)
 
 
+def mm_tn(left, right):
+    return lax.dot_general(left, right, (((0,), (0,)), ((), ())), preferred_element_type=WIDE)
+
+
 def row_mean(block):
     return jnp.sum(block, axis=-1, keepdims=True) * (1.0 / block.shape[-1])
 
 
 def gelu_parts(value):
-    size = jnp.abs(value)
-    bell = jnp.exp(value * value * -0.5)
-    t = 1.0 / (1.0 + size * (0.3275911 * 0.7071067811865476))
-    series = t * (
-        0.5 * 0.254829592
-        + t
-        * (
-            0.5 * -0.284496736
-            + t * (0.5 * 1.421413741 + t * (0.5 * -1.453152027 + t * (0.5 * 1.061405429)))
-        )
-    )
-    tail = series * bell
-    below = jnp.where(value < 0.0, tail, 1.0 - tail)
-    return value * below, below + value * bell * 0.3989422804014327
+    below = 0.5 + 0.5 * lax.erf(value * 0.7071067811865476)
+    bell = jnp.exp(value * value * -0.5) * 0.3989422804014327
+    return value * below, below + value * bell
 
 
 def pair_select(low, high):
@@ -184,19 +180,24 @@
 def kernel(plan, *refs):
     if plan is not None:
         (x_ref, gout_ref, wq_ref, wk_ref, wv_ref, wo_ref, up_ref, down_ref, dq_ref, dv_ref, uq_ref, uv_ref) = refs[:12]
-        (bq_ref, bv_ref, bup_ref, vec_ref, down_t_ref, seg_ref, live_ref) = refs[12:19]
-        (out_ref, gin_ref, glq_ref, glv_ref) = refs[19:23]
-        (wq, wk, wv, wo, q, k, v, probs, ctx, n1, s1, act, slope, acc, mask, u_t) = refs[23:39]
-        (a_ref, b_ref, c_ref, bias, biases, part, near, far) = refs[39:47]
-        (send, recv, bias_send, bias_recv, near_send, near_recv, far_send, far_recv) = refs[47:]
+        (bq_ref, bv_ref, bup_ref) = refs[12:15]
+        vector_refs, (seg_ref, live_ref) = refs[15:21], refs[21:23]
+        (out_ref, gin_ref, glq_ref, glv_ref) = refs[23:27]
+        (wq, wk, wv, wo, q, k, v, probs, ctx, n1, s1, act, slope, acc, mask, u_t) = refs[27:43]
+        (a_ref, b_ref, c_ref, bias, biases, part, near, far) = refs[43:51]
+        (send, recv, bias_send, bias_recv, near_send, near_recv, far_send, far_recv) = refs[51:]
     else:
-        (x_ref, gout_ref, a_ref, b_ref, c_ref, biases_ref, vec_ref, down_t_ref, seg_ref, live_ref) = refs[:10]
-        (out_ref, gin_ref, gl_ref) = refs[10:13]
-        (wq, wk, wv, wo, q, k, v, probs, ctx, n1, s1, act, slope, acc, mask, u_t, biases) = refs[13:]
+        (x_ref, gout_ref, a_ref, b_ref, c_ref, biases_ref, dq_ref, dv_ref) = refs[:8]
+        vector_refs, (seg_ref, live_ref) = refs[8:14], refs[14:16]
+        (out_ref, gin_ref, gl_ref) = refs[16:19]
+        (wq, wk, wv, wo, q, k, v, probs, ctx, n1, s1, act, slope, acc, mask, u_t, biases) = refs[19:]
     rows, width = x_ref.shape
     seqs = rows // SEQ
     pairs = width // LANES
     groups = a_ref.shape[0]
+    out_bias, down_bias, gain1, shift1, gain2, shift2 = (
+        jnp.reshape(ref[...], (1, width)) for ref in vector_refs
+    )
 
     if plan is not None:
         gather = Gather((a_ref, b_ref, c_ref), send, recv)
@@ -213,9 +214,11 @@
             pl.semaphore_signal(barrier, inc=1, device_id=(other, me_t), device_id_type=BY_MESH)
 
         mine = pl.ds(pl.multiple_of(me_d * depth, depth), depth)
-        query = wq_ref[...].astype(WIDE) + ADAPTER_SCALE * mm(dq_ref[mine, :], uq_ref[...])
-        query = query * SCORE_SCALE
-        value = wv_ref[...].astype(WIDE) + ADAPTER_SCALE * mm(dv_ref[mine, :], uv_ref[...])
+        across = wq_ref.shape[1]
+        acc[0:width, 0:across] = mm_tn(dq_ref[...], uq_ref[...])
+        acc[0:width, 256 : 256 + across] = mm_tn(dv_ref[...], uv_ref[...])
+        query = (wq_ref[...].astype(WIDE) + ADAPTER_SCALE * acc[mine, 0:across]) * SCORE_SCALE
+        value = wv_ref[...].astype(WIDE) + ADAPTER_SCALE * acc[mine, 256 : 256 + across]
         key = wk_ref[...].astype(WIDE)
         out_t = jnp.transpose(wo_ref[...].astype(WIDE))
         a_ref[me_t, mine, 0:128] = query[:, 0:128].astype(NARROW)
@@ -224,9 +227,9 @@
         a_ref[me_t, mine, 384:512] = jnp.concatenate([query[:, 128:], key[:, 128:]], axis=1).astype(NARROW)
         a_ref[me_t, mine, 512:640] = jnp.concatenate([value[:, 128:], out_t[:, 128:]], axis=1).astype(NARROW)
         a_ref[me_t, mine, 640:768] = out_t[:, 0:128].astype(NARROW)
-        bias[me_t, 0:1, :] = bup_ref[...]
-        bias[me_t, 1:2, 0:192] = bq_ref[...] * SCORE_SCALE
-        bias[me_t, 1:2, 256:448] = bv_ref[...]
+        bias[me_t, 0:1, :] = jnp.reshape(bup_ref[...], (1, width))
+        bias[me_t, 1:2, 0:across] = jnp.reshape(bq_ref[...], (1, across)) * SCORE_SCALE
+        bias[me_t, 1:2, 256 : 256 + across] = jnp.reshape(bv_ref[...], (1, across))
         pl.semaphore_wait(barrier, len(others_t) + len(others_d))
 
         def bias_copy(i):
@@ -242,7 +245,7 @@
         for name in ("own",):
             gather.step(0, name)
         b_ref[me_t, mine, :] = up_ref[...]
-        c_ref[me_t, mine, :] = jnp.transpose(down_ref[...].astype(WIDE)).astype(NARROW)
+        c_ref[me_t, mine, :] = down_ref[...]
         for i in range(len(others_t)):
             bias_copy(i).start()
     else:
@@ -289,7 +292,8 @@
                 at = SPAN_STARTS[block] + j * LANES
                 mask[seq, at : at + LANES, :] = jnp.where(seen, 0.0, NEG_FILL)
 
-    u_t[...] = mm_nt(down_t_ref[...], x_ref[...]).astype(NARROW)
+    adapters_down = jnp.concatenate([dq_ref[...].astype(WIDE), dv_ref[...].astype(WIDE)], axis=0)
+    u_t[...] = mm_nt(adapters_down.astype(NARROW), x_ref[...]).astype(NARROW)
 
     ticks("masked")
 
@@ -343,6 +347,8 @@
     lax.fori_loop(0, width // 256, project, 0)
 
     lane = lax.broadcasted_iota(jnp.int32, (LANES, LANES), 1)
+    together = 3
+    steps = seqs * pairs // together
 
     def stacked(tile):
         none = jnp.zeros_like(tile)
@@ -350,46 +356,52 @@
             [jnp.where(lane < HEAD_DIM, tile, none), jnp.where(lane < HEAD_DIM, none, tile)], axis=0
         )
 
-    def turned(tile):
-        own = jnp.concatenate([tile[:HEAD_DIM, :LANES], tile[HEAD_DIM:, LANES:]], axis=0)
-        return jnp.transpose(own)
+    def merged(tile):
+        return jnp.where(lane < HEAD_DIM, tile[:LANES], tile[LANES:]).astype(NARROW)
+
+    def work_of(step):
+        items = []
+        for one in range(together):
+            index = step * together + one
+            seq = index // pairs
+            base = pl.multiple_of(seq * SEQ, SEQ)
+            at = pl.ds(pl.multiple_of((index - seq * pairs) * LANES, LANES), LANES)
+            for block, (start, stop) in enumerate(KEY_SPANS):
+                here = pl.ds(base + block * LANES, LANES)
+                there = pl.ds(base + start, stop - start)
+                span = pl.ds(SPAN_STARTS[block], stop - start)
+                items.append((index, seq, here, there, at, span, block))
+        return items
 
     def attend(step, carry):
         ticks("attend", step)
-        seq = step // pairs
-        pair = step - seq * pairs
-        at = pl.ds(pl.multiple_of(pair * LANES, LANES), LANES)
-        base = pl.multiple_of(seq * SEQ, SEQ)
-        everything = pl.ds(base, SEQ)
-        keys = k[everything, at]
-        values_t = jnp.transpose(v[everything, at].astype(WIDE)).astype(NARROW)
-        for block, (start, stop) in enumerate(KEY_SPANS):
-            here = pl.ds(base + block * LANES, LANES)
-            scores = mm_nt(keys[start:stop], stacked(q[here, at]))
-            span = pl.ds(SPAN_STARTS[block], stop - start)
+        items = work_of(step)
+        scores = [mm_nt(k[there, at], stacked(q[here, at])) for _, _, here, there, at, _, _ in items]
+        weights = []
+        for (index, seq, _, _, _, span, block), score in zip(items, scores):
             if block:
                 shade = mask[seq, span, :]
-                scores = scores + jnp.concatenate([shade, shade], axis=1)
-            top = jnp.max(scores, axis=0, keepdims=True)
-            powers = jnp.exp(scores - top)
+                score = score + jnp.concatenate([shade, shade], axis=1)
+            powers = jnp.exp(score - jnp.max(score, axis=0, keepdims=True))
             total = jnp.sum(powers, axis=0, keepdims=True)
-            weights = (powers * (1.0 / total)).astype(NARROW)
-            probs[step, span, :] = weights
-            ctx[here, at] = turned(mm(values_t[:, start:stop], weights)).astype(NARROW)
+            weights.append((powers * (1.0 / total)).astype(NARROW))
+            probs[index, span, :] = weights[-1]
+        for (_, _, here, there, at, _, _), weight in zip(items, weights):
+            ctx[here, at] = merged(mm_tn(weight, v[there, at]))
         return carry
 
-    lax.fori_loop(0, seqs * pairs, attend, 0)
+    lax.fori_loop(0, steps, attend, 0)
 
     def first_norm(step, carry):
         ticks("first_norm", step)
         at = pl.ds(pl.multiple_of(step * 256, 256), 256)
-        r = x_ref[at, :].astype(WIDE) + (mm_nt(ctx[at, :], wo[...]) + vec_ref[0:1, :])
+        r = x_ref[at, :].astype(WIDE) + (mm_nt(ctx[at, :], wo[...]) + out_bias)
         centered = r - row_mean(r)
         inverse = lax.rsqrt(row_mean(centered * centered) + EPSILON)
         normed = centered * inverse
         n1[at, :] = normed
         s1[at, :] = inverse
-        out_ref[at, :] = (normed * vec_ref[2:3, :] + vec_ref[3:4, :]).astype(NARROW)
+        out_ref[at, :] = (normed * gain1 + shift1).astype(NARROW)
         return carry
 
     lax.fori_loop(0, rows // 256, first_norm, 0)
@@ -411,14 +423,14 @@
 
     def second_norm(step, carry):
         at = pl.ds(pl.multiple_of(step * 256, 256), 256)
-        r = n1[at, :] * vec_ref[2:3, :] + vec_ref[3:4, :] + vec_ref[1:2, :]
+        r = n1[at, :] * gain1 + shift1 + down_bias
         for group in range(groups):
             r = r + mm_nt(act[at, group * width : (group + 1) * width], c_ref[group])
         centered = r - row_mean(r)
         inverse = lax.rsqrt(row_mean(centered * centered) + EPSILON)
         normed = centered * inverse
-        out_ref[at, :] = (normed * vec_ref[4:5, :] + vec_ref[5:6, :]).astype(NARROW)
-        e = gout_ref[at, :].astype(WIDE) * vec_ref[4:5, :]
+        out_ref[at, :] = (normed * gain2 + shift2).astype(NARROW)
+        e = gout_ref[at, :].astype(WIDE) * gain2
         acc[at, :] = inverse * (e - row_mean(e) - normed * row_mean(e * normed))
         return carry
 
@@ -434,7 +446,7 @@
             grad = (mm(low, c_ref[group]) * slope[at, cols].astype(WIDE)).astype(NARROW)
             total = total + mm_nt(grad, b_ref[group])
         normed = n1[at, :]
-        e = total * vec_ref[2:3, :]
+        e = total * gain1
         first = s1[at, :] * (e - row_mean(e) - normed * row_mean(e * normed))
         acc[at, :] = first
         ctx[at, :] = mm(first.astype(NARROW), wo[...]).astype(NARROW)
@@ -443,41 +455,32 @@
     lax.fori_loop(0, rows // 256, down_back, 0)
 
     def attend_back(step, carry):
-        seq = step // pairs
-        pair = step - seq * pairs
-        at = pl.ds(pl.multiple_of(pair * LANES, LANES), LANES)
-        base = pl.multiple_of(seq * SEQ, SEQ)
-        everything = pl.ds(base, SEQ)
-        keys = k[everything, at]
-        values = v[everything, at]
-        keys_t = jnp.transpose(keys.astype(WIDE)).astype(NARROW)
-        grad_k = [None] * 4
-        grad_v = [None] * 4
-        for block, (start, stop) in enumerate(KEY_SPANS):
-            here = pl.ds(base + block * LANES, LANES)
+        items = work_of(step)
+        grad_q, grad_k, grad_v = [], {}, {}
+        for index, seq, here, there, at, span, block in items:
             grads = stacked(ctx[here, at])
-            span = pl.ds(SPAN_STARTS[block], stop - start)
-            weights = probs[step, span, :]
-            part = weights.astype(WIDE) * mm_nt(values[start:stop], grads)
+            weights = probs[index, span, :]
+            part = weights.astype(WIDE) * mm_nt(v[there, at], grads)
             inside = jnp.sum(part, axis=0, keepdims=True)
             grad_scores = (part - weights.astype(WIDE) * inside).astype(NARROW)
+            grad_q.append(merged(mm_tn(grad_scores, k[there, at])))
             for_keys = mm(grad_scores, stacked(q[here, at]))
             for_values = mm(weights, grads)
-            q[here, at] = turned(mm(keys_t[:, start:stop], grad_scores)).astype(NARROW)
+            start, stop = KEY_SPANS[block]
             for j in range((stop - start) // LANES):
-                kb = start // LANES + j
                 rows_here = slice(j * LANES, (j + 1) * LANES)
-                grad_k[kb] = for_keys[rows_here] if grad_k[kb] is None else grad_k[kb] + for_keys[rows_here]
-                grad_v[kb] = (
-                    for_values[rows_here] if grad_v[kb] is None else grad_v[kb] + for_values[rows_here]
-                )
-        for kb in range(4):
-            here = pl.ds(base + kb * LANES, LANES)
-            k[here, at] = grad_k[kb].astype(NARROW)
-            v[here, at] = grad_v[kb].astype(NARROW)
+                key = (len(grad_q) - 1) // 4, start // LANES + j
+                for grad, more in ((grad_k, for_keys), (grad_v, for_values)):
+                    grad[key] = grad[key] + more[rows_here] if key in grad else more[rows_here]
+        for (_, _, here, _, at, _, _), grad in zip(items, grad_q):
+            q[here, at] = grad
+        for one, kb in grad_k:
+            _, _, here, _, at, _, _ = items[4 * one + kb]
+            k[here, at] = grad_k[one, kb].astype(NARROW)
+            v[here, at] = grad_v[one, kb].astype(NARROW)
         return carry
 
-    lax.fori_loop(0, seqs * pairs, attend_back, 0)
+    lax.fori_loop(0, steps, attend_back, 0)
 
     grad_q = mm(u_t[0:8, :], q[...]) * (ADAPTER_SCALE * SCORE_SCALE)
     grad_v = mm(u_t[8:16, :], v[...]) * ADAPTER_SCALE
@@ -577,7 +580,7 @@
     ]
 
 
-def run_layer(x, gout, a, b, c, biases, vectors, down_t, seg, live):
+def run_layer(x, gout, a, b, c, biases, downs, vectors, seg, live):
     rows, width = x.shape
     shape = jax.ShapeDtypeStruct
     hidden = b.shape[0] * b.shape[2]
@@ -588,21 +591,21 @@
             shape((rows, width), NARROW),
             shape((2 * ADAPTER_RANK, width), WIDE),
         ),
-        in_specs=[pl.BlockSpec(memory_space=pltpu.VMEM)] * 10,
+        in_specs=[pl.BlockSpec(memory_space=pltpu.VMEM)] * 16,
         out_specs=[pl.BlockSpec(memory_space=pltpu.VMEM)] * 3,
         scratch_shapes=scratch(rows, width, hidden) + [pltpu.VMEM((8, width), WIDE)],
         compiler_params=pltpu.CompilerParams(vmem_limit_bytes=63 << 20),
-    )(x, gout, a, b, c, biases, vectors, down_t, seg, live)
-
-
-def run_layer_and_gather(x, gout, blocks, adapters, biases, vectors, down_t, seg, live):
+    )(x, gout, a, b, c, biases, *downs, *vectors, seg, live)
+
+
+def run_layer_and_gather(x, gout, blocks, adapters, biases, vectors, seg, live):
     rows, width = x.shape
     groups = width // blocks[0].shape[1]
     dps = width // blocks[0].shape[0]
     shape = jax.ShapeDtypeStruct
     gathered = pltpu.VMEM((groups, width, width), NARROW)
     signals = pltpu.SemaphoreType.DMA
-    operands = (x, gout, *blocks, *adapters, *biases, vectors, down_t, seg, live)
+    operands = (x, gout, *blocks, *adapters, *biases, *vectors, seg, live)
     return pl.pallas_call(
         functools.partial(kernel, PLAN),
         out_shape=(
@@ -680,28 +683,25 @@
     rows, width = layer_input_rows.shape
     depth, across = query_weight.shape
     groups = width // across
-    vectors = jnp.stack(
-        [
-            output_bias_vector,
-            down_bias_vector,
-            first_norm_gain,
-            first_norm_bias,
-            second_norm_gain,
-            second_norm_bias,
-        ]
+    vectors = (
+        output_bias_vector,
+        down_bias_vector,
+        first_norm_gain,
+        first_norm_bias,
+        second_norm_gain,
+        second_norm_bias,
     )
-    down_t = jnp.concatenate([query_down_frozen, value_down_frozen], axis=1).T
+    downs = (query_down_frozen.T, value_down_frozen.T)
     segment_rows = segments.reshape(-1, LANES)
     live_rows = sentence_row_mask.reshape(-1, LANES)
     if grid == (8, 4):
         return run_layer_and_gather(
             layer_input_rows,
             output_gradient,
-            (query_weight, key_weight, value_weight, output_weight, up_weight, down_weight),
-            (query_down_frozen, value_down_frozen, query_up_trained, value_up_trained),
-            (query_bias_vector[None], value_bias_vector[None], up_bias_vector[None]),
+            (query_weight, key_weight, value_weight, output_weight, up_weight, down_weight.T),
+            (*downs, query_up_trained, value_up_trained),
+            (query_bias_vector, value_bias_vector, up_bias_vector),
             vectors,
-            down_t,
             segment_rows,
             live_rows,
         )
@@ -742,7 +742,7 @@
     seg = lax.dynamic_slice_in_dim(segment_rows, place * blocks, blocks)
     live = lax.dynamic_slice_in_dim(live_rows, place * blocks, blocks)
     output, grad_input, grads = run_layer(
-        layer_input_rows, output_gradient, a, b, c, biases, vectors, down_t, seg, live
+        layer_input_rows, output_gradient, a, b, c, biases, downs, vectors, seg, live
     )
     grads = from_pairs(lax.psum(grads, everyone), groups)
     grads = lax.dynamic_slice_in_dim(grads, place * across, across, axis=1)

time: 182 us -> 139 us (0.76)
  Pallas kernels: 163 us -> 133 us
  local copies, waits for them, and re-layouts: 15.9 us -> 5.12 us
    pallas_call x1, Pallas kernels: 163 us -> 133 us  [run_layer_and_gather(): pl.pallas_call(functools.partial(kernel, PLAN), out_shape=(shape((rows, w...]
    unnamed x13 -> x10, local copies, waits for them, and re-layouts: 9.89 us -> 5.12 us
    another operation x7 -> x0, local copies, waits for them, and re-layouts: 4.76 us -> none  [body(): jnp.stack([output_bias_vector, down_bias_vector, first_norm_gain, first_n...]
where the time goes in v4:
time: 139 us
  Pallas kernels  133 us (96%)
  local copies, waits for them, and re-layouts  5.12 us (4%)
    pallas_call x1, Pallas kernels, run_layer_and_gather(): pl.pallas_call(functools.partial(kernel, PLAN), out_shape=(shape((rows, w...  133 us
    unnamed x10, local copies, waits for them, and re-layouts  5.12 us

profile of v4, /device:TPU:0, one launch (start us, length us, event | category | flops | bytes accessed | tf_op | source)
XLA Modules:
  0.0 139.1 jit_solution(16630707552451862762)
XLA Ops:
  0.6 133.3 %shard_map.246 = (bf16[1024,768]{1,0:T(8,128)(2,1)}, bf16[1024,768]{1,0:T(8,128)(2,1)}, f32[8,192]{1,0:T(8,128)}, f32[8,192]{1,0:T(8,128)}) custom-call(bf16[1024,768]{1,0:T(8,128)(2,1)} %refs_0_.1, bf16[1024,768]{1,0:T(8,128)(2,1)} %refs_1_.1, bf16[96,192]{1,0:T(8,128)(2,1)} %refs_2_.1, bf16[96,192]{1,0:T(8,128)(2,1)} %refs_3_.1, bf16[96,192]{1,0:T(8,128)(2,1)} %refs_4_.1, ...), custom_call_target="tpu_custom_call" | custom-call | tf_op jit(solution)/shard_map/pallas_call | solution.py:609
  134.0 0.0 copy-start
  134.0 2.8 %copy.31 = bf16[1024,768]{1,0:T(8,128)(2,1)} copy(bf16[1024,768]{1,0:T(8,128)(2,1)} %get-tuple-element.8) | data formatting | bytes 3145728
  136.7 0.0 copy-done
  136.7 0.0 copy-start.2
  136.7 0.0 copy-start.1
  136.7 1.1 copy.32
  137.9 0.0 copy-done.2
  137.9 0.6 copy.33
  138.5 0.0 copy-done.1
  138.5 0.6 copy.34
Async XLA Ops:
  134.0 2.8 %copy-start = (bf16[1024,768]{1,0:T(8,128)(2,1)S(1)}, bf16[1024,768]{1,0:T(8,128)(2,1)}, u32[]{:S(2)}) copy-start(bf16[1024,768]{1,0:T(8,128)(2,1)} %get-tuple-element.9) | copy-start | bytes 4718596
  136.7 1.1 copy-start.2
  136.7 1.7 %copy-start.1 = (f32[8,192]{1,0:T(8,128)S(1)}, f32[8,192]{1,0:T(8,128)}, u32[]{:S(2)}) copy-start(f32[8,192]{1,0:T(8,128)} %get-tuple-element.11) | copy-start | bytes 18436

commit v5 on v4

--- a/solution.py
+++ b/solution.py
@@ -24,50 +24,109 @@
 SPAN_TOTAL = 1024
 BY_MESH = pl.DeviceIdType.MESH
 
+AWAY = {"u1": 3, "u2": 2, "u3": 1, "d1": 1, "d2": 2, "d3": 3}
 ARRIVALS = (
-    ("Z1", "Z2", "Z3", "X0", "X1", "X2", "X3", "Y0", "Y1", "Y2", "Y3")
-    + ("D0a", "D0b", "D1", "D2a", "D2b", "D3", "C")
-    + tuple("C" + kind + str(k) for kind in "ZXYD" for k in range(4) if kind + str(k) != "Z0")
+    ("X0", "Y0", "D0a", "D0b", "C", "CX0", "CY0", "CD0")
+    + tuple(kind + str(k) for kind in ("Z", "X", "Y", "CZ", "CX", "CY", "CD") for k in (1, 2, 3))
+    + tuple("D" + str(k) + half for k in (1, 2, 3) for half in "ab")
 )
-SIGNALS = {name: i for i, name in enumerate(ARRIVALS + ("Z2down",))}
+SIGNALS = {name: i for i, name in enumerate(ARRIVALS)}
+for name in tuple(kind + str(k) for kind in "ZXY" for k in (1, 2, 3)):
+    SIGNALS[name + "-"] = len(SIGNALS)
+FROM_CORE = tuple(name for name in ARRIVALS if name[0] == "C")
 PASS_ON = {
-    "own": (("X0", "x", ""), ("Y0", "y", ""), ("Z1", "up", ""), ("Z3", "down", ""), ("C", "core", "")),
-    "X0": (("X1", "up", ""), ("D0b", "y", "b"), ("CX0", "core", "")),
-    "Y0": (("Y3", "down", ""), ("D0a", "x", "a"), ("CY0", "core", "")),
-    "Z1": (("Y1", "y", ""), ("CZ1", "core", "")),
-    "Z3": (("X3", "x", ""), ("CZ3", "core", "")),
-    "X1": (("CX1", "core", ""),),
-    "Y3": (("CY3", "core", ""),),
-    "Z2": (("X2", "x", ""), ("Y2", "y", ""), ("CZ2", "core", "")),
-    "Y1": (("D1", "x", ""), ("CY1", "core", "")),
-    "X3": (("D3", "y", ""), ("CX3", "core", "")),
-    "X2": (("D2b", "y", "b"), ("CX2", "core", "")),
-    "Y2": (("D2a", "x", "a"), ("CY2", "core", "")),
-    "D0b": (("CD0", "core", ""),),
-    "D1": (("CD1", "core", ""),),
-    "D2b": (("CD2", "core", ""),),
-    "D3": (("CD3", "core", ""),),
+    "own": [("X0", "x", ""), ("Y0", "y", ""), ("C", "core", "")],
+    "ownz": [("Zd1", "+", ""), ("Zu1", "-", "")],
+    "X0": [("D0b", "y", "b"), ("CX0", "core", "")],
+    "X0z": [("Xd1", "+", ""), ("Xu1", "-", "")],
+    "Y0": [("D0a", "x", "a"), ("CY0", "core", "")],
+    "Y0z": [("Yd1", "+", ""), ("Yu1", "-", "")],
+    "D0a": [],
+    "D0b": [("CD0", "core", "")],
 }
-ROUNDS = (
-    ("own",),
-    ("X0", "Y0", "Z1", "Z3"),
-    ("X1", "Y3", "Z2", "Y1", "X3"),
-    ("X2", "Y2", "D0a", "D0b", "D1", "D3"),
-    ("D2a", "D2b"),
-    tuple(name for name in ARRIVALS if name[0] == "C"),
-)
-
-
-def in_rounds(*rounds):
-    return [(group, name) for number, group in rounds for name in ROUNDS[number]]
+for away in AWAY:
+    onward = "Z" + away[0] + str(int(away[1]) + 1)
+    spread_z = [(onward, "+" if away[0] == "d" else "-", "")] if away[1] < "3" else []
+    spread_xy = [("X" + away, "x", ""), ("Y" + away, "y", "")] if away[1] > "1" else []
+    PASS_ON["Z" + away] = spread_z + spread_xy + [("CZ" + away, "core", "")]
+    PASS_ON["X" + away] = [("D" + away + "b", "y", "b"), ("CX" + away, "core", "")]
+    PASS_ON["Y" + away] = [("D" + away + "a", "x", "a"), ("CY" + away, "core", "")]
+    PASS_ON["D" + away + "a"] = []
+    PASS_ON["D" + away + "b"] = [("CD" + away, "core", "")]
+
+
+STEPS = tuple(PASS_ON)
+
+
+def steps_of(*codes):
+    return [(code // 100, STEPS[code % 100]) for code in codes]
 
 
 PLAN = {
-    "start": {0: in_rounds((1, 0), (0, 1), (2, 0), (1, 1), (3, 0), (0, 2), (4, 0), (5, 0))},
-    "project": {0: in_rounds((2, 1)), 1: in_rounds((1, 2)), 2: in_rounds((3, 1))},
-    "attend": {0: in_rounds((2, 2)), 1: in_rounds((4, 1), (3, 2)), 2: in_rounds((4, 2))},
-    "before up": {0: in_rounds((5, 1))},
-    "before down": {0: in_rounds((5, 2))},
+    "first": {
+        0: steps_of(
+            1, 0,
+        ),
+    },
+    "start": {
+        0: steps_of(
+            100, 101, 8, 4, 2, 200, 23, 5, 6, 102, 13, 28, 25, 204, 3, 29, 18, 14, 33, 10, 30,
+            108, 15, 19, 20, 123, 24, 7, 11, 9, 201, 113, 34, 35, 16, 17, 202,
+        ),
+    },
+    "masked": {
+        0: steps_of(
+            128, 26, 12, 21, 22, 36, 37, 27, 104, 31, 32, 206,
+        ) + [(0, name) for name in FROM_CORE],
+    },
+    "project": {
+        0: steps_of(
+            208, 130, 133, 118, 223, 103,
+        ),
+        1: steps_of(
+            105,
+        ),
+        2: steps_of(
+            228, 114,
+        ),
+    },
+    "attend": {
+        0: steps_of(
+            213, 119, 129,
+        ),
+        2: steps_of(
+            115, 230, 203, 205, 120, 134,
+        ),
+        3: steps_of(
+            125, 109, 135, 110, 124,
+        ),
+    },
+    "first_norm": {
+        2: steps_of(
+            126, 231, 116, 117, 121, 106, 107, 229, 218, 127,
+        ),
+        3: steps_of(
+            122, 136, 137, 214, 111, 112, 233, 215, 131, 132,
+        ),
+    },
+    "before up": {
+        0: steps_of(
+
+        ) + [(1, name) for name in FROM_CORE],
+    },
+    "up": {
+        1: steps_of(
+            219, 235, 234, 207, 220, 225, 216, 209, 217, 210, 224, 232,
+        ),
+        3: steps_of(
+            221, 222, 211, 212, 226, 227, 236, 237,
+        ),
+    },
+    "before down": {
+        0: steps_of(
+
+        ) + [(2, name) for name in FROM_CORE],
+    },
 }
 
 
@@ -80,74 +139,92 @@
         self.tx = lax.rem(self.t + 2, 4)
         self.tc = self.t + 1 - 2 * lax.rem(self.t, 2)
         self.txc = lax.rem(self.tc + 2, 4)
-        self.middle = (self.z == 1) | (self.z == 2)
 
     def peer(self, kind):
         return {
             "x": (self.d, self.tx),
             "y": (self.z * 2 + 1 - self.y, self.t),
             "core": (self.d, self.tc),
-            "up": (lax.rem(self.z + 1, 4) * 2 + self.y, self.t),
-            "down": (lax.rem(self.z + 3, 4) * 2 + self.y, self.t),
+            "+": (self.d + 2, self.t),
+            "-": (self.d - 2, self.t),
         }[kind]
 
+    def there_is(self, kind):
+        if kind[0] in "+u":
+            return self.z <= 3 - int(kind[1:] or 1)
+        if kind[0] in "-d":
+            return self.z >= int(kind[1:] or 1)
+        return None
+
+    @staticmethod
+    def away(name):
+        for away, k in AWAY.items():
+            if away in name:
+                return away, name.replace(away, str(k))
+        return None, name
+
     def part(self, group, name, half=""):
-        if name == "own":
+        away, signal = self.away(name)
+        if name.startswith("own"):
             dp, t = self.d, self.t
         elif name == "C":
             dp, t = self.d, self.tc
         else:
-            kind = name[-2] if name[-1].isdigit() else name[-3]
-            k = int(name[-1] if name[-1].isdigit() else name[-2])
-            half = half or (name[-1] if not name[-1].isdigit() else "")
+            bare = signal.rstrip("abz")
+            half = half or signal[len(bare) :].strip("z")
+            kind, k = bare[-2], int(bare[-1])
+            if away:
+                plane = self.z + int(away[1]) if away[0] == "u" else self.z - int(away[1])
+            else:
+                plane = lax.rem(self.z - k + 4, 4) if k else self.z
             near, far = (self.tc, self.txc) if name[0] == "C" else (self.t, self.tx)
-            dp = lax.rem(self.z - k + 4, 4) * 2 + (self.y if kind in "ZX" else 1 - self.y)
+            dp = plane * 2 + (self.y if kind in "ZX" else 1 - self.y)
             t = near if kind in "ZY" else far
         size = self.depth // 2 if half else self.depth
         first = dp * self.depth + (size if half == "b" else 0)
         return self.blocks[group].at[t, pl.ds(pl.multiple_of(first, 16), size), :]
 
-    def copy(self, group, part, name, to, sender=None):
+    def copy(self, group, part, name, to):
+        signal = self.away(name)[1]
         return pltpu.make_async_remote_copy(
             src_ref=part,
             dst_ref=part,
-            send_sem=self.send.at[group, SIGNALS[sender or name]],
-            recv_sem=self.recv.at[group, SIGNALS[name]],
+            send_sem=self.send.at[group, SIGNALS[signal + "-" if to == "-" else signal]],
+            recv_sem=self.recv.at[group, SIGNALS[signal]],
             device_id=self.peer(to),
             device_id_type=BY_MESH,
         )
 
-    def outgoing(self, group, name):
-        whole = name[:2] if name[0] == "D" else name
-        return [
-            self.copy(group, self.part(group, whole, half), out, to)
-            for out, to, half in PASS_ON.get(name, ())
-        ]
-
-    def relayed(self, group, name):
-        to, sender = ("up", "Z2") if name == "Z1" else ("down", "Z2down")
-        return self.copy(group, self.part(group, name), "Z2", to, sender)
+    def when(self, kind, body):
+        there = self.there_is(kind) if kind else None
+        if there is None:
+            body()
+        else:
+            pl.when(there)(body)
+
+    def each_copy(self, group, name, act):
+        for out, to, half in PASS_ON.get(name, ()):
+            source = name[:-1] if name[0] == "D" else name
+
+            def one(out=out, to=to, half=half, source=source):
+                act(self.copy(group, self.part(group, source, half), out, to))
+
+            self.when(to, one)
 
     def step(self, group, name):
-        if name != "own":
-            self.copy(group, self.part(group, name), name, "x").wait_recv()
-        for copy in self.outgoing(group, name):
-            copy.start()
-        if name in ("Z1", "Z3"):
-
-            @pl.when(self.middle)
-            def _():
-                self.relayed(group, name).start()
+        def body():
+            if not name.startswith("own") and not name.endswith("z"):
+                self.copy(group, self.part(group, name), name, "x").wait_recv()
+            self.each_copy(group, name, lambda copy: copy.start())
+
+        self.when(self.away(name)[0], body)
 
     def finish(self, group):
         for name in PASS_ON:
-            for copy in self.outgoing(group, name):
-                copy.wait_send()
-
-        @pl.when(self.middle)
-        def _():
-            self.relayed(group, "Z1").wait_send()
-            self.relayed(group, "Z3").wait_send()
+            self.when(
+                self.away(name)[0],
+                lambda name=name: self.each_copy(group, name, lambda copy: copy.wait_send()),
+            )
 
 
 def mm(left, right):
@@ -242,8 +319,8 @@
                 device_id_type=BY_MESH,
             )
 
-        for name in ("own",):
-            gather.step(0, name)
+        for group, name in plan.get("first", {0: ()})[0]:
+            gather.step(group, name)
         b_ref[me_t, mine, :] = up_ref[...]
         c_ref[me_t, mine, :] = down_ref[...]
         for i in range(len(others_t)):
@@ -602,17 +679,16 @@
     rows, width = x.shape
     groups = width // blocks[0].shape[1]
     dps = width // blocks[0].shape[0]
-    shape = jax.ShapeDtypeStruct
     gathered = pltpu.VMEM((groups, width, width), NARROW)
     signals = pltpu.SemaphoreType.DMA
     operands = (x, gout, *blocks, *adapters, *biases, *vectors, seg, live)
     return pl.pallas_call(
         functools.partial(kernel, PLAN),
         out_shape=(
-            shape((rows, width), NARROW),
-            shape((rows, width), NARROW),
-            shape((ADAPTER_RANK, width // groups), WIDE),
-            shape((ADAPTER_RANK, width // groups), WIDE),
+            pltpu.VMEM((rows, width), NARROW),
+            pltpu.VMEM((rows, width), NARROW),
+            pltpu.VMEM((ADAPTER_RANK, width // groups), WIDE),
+            pltpu.VMEM((ADAPTER_RANK, width // groups), WIDE),
         ),
         in_specs=[pl.BlockSpec(memory_space=pltpu.VMEM)] * len(operands),
         out_specs=[pl.BlockSpec(memory_space=pltpu.VMEM)] * 4,
@@ -636,7 +712,7 @@
             signals((dps - 1,)),
         ],
         compiler_params=pltpu.CompilerParams(
-            collective_id=0, has_side_effects=True, vmem_limit_bytes=63 << 20
+            collective_id=0, has_side_effects=True, vmem_limit_bytes=59 << 20
         ),
     )(*operands)
 

time: 139 us -> 118 us (0.85)
  Pallas kernels: 133 us -> 114 us
  local copies, waits for them, and re-layouts: 5.12 us -> 3.48 us
    pallas_call x1, Pallas kernels: 133 us -> 114 us  [run_layer_and_gather(): pl.pallas_call(functools.partial(kernel, PLAN), out_shape=(pltpu.VMEM((ro...]
    unnamed x10 -> x4, local copies, waits for them, and re-layouts: 5.12 us -> 3.48 us
where the time goes in v5:
time: 118 us
  Pallas kernels  114 us (97%)
  local copies, waits for them, and re-layouts  3.48 us (3%)
    pallas_call x1, Pallas kernels, run_layer_and_gather(): pl.pallas_call(functools.partial(kernel, PLAN), out_shape=(pltpu.VMEM((ro...  114 us
    unnamed x4, local copies, waits for them, and re-layouts  3.48 us

profile of v5, /device:TPU:0, one launch (start us, length us, event | category | flops | bytes accessed | tf_op | source)
XLA Modules:
  0.0 118.2 jit_solution(16501563339650981332)
XLA Ops:
  0.6 114.0 %shard_map.246 = (bf16[1024,768]{1,0:T(8,128)(2,1)S(1)}, bf16[1024,768]{1,0:T(8,128)(2,1)S(1)}, f32[8,192]{1,0:T(8,128)S(1)}, f32[8,192]{1,0:T(8,128)S(1)}) custom-call(bf16[1024,768]{1,0:T(8,128)(2,1)} %refs_0_.1, bf16[1024,768]{1,0:T(8,128)(2,1)} %refs_1_.1, bf16[96,192]{1,0:T(8,128)(2,1)} %refs_2_.1, bf16[96,192]{1,0:T(8,128)(2,1)} %refs_3_.1, ...), custom_call_target="tpu_custom_call" | custom-call | tf_op jit(solution)/shard_map/pallas_call | solution.py:685
  114.7 1.1 copy.31
  115.8 0.6 copy.33
  116.4 0.6 copy.34
  117.0 1.1 copy.32

commit v6 on v5

--- a/solution.py
+++ b/solution.py
@@ -256,13 +256,14 @@
 
 def kernel(plan, *refs):
     if plan is not None:
-        (x_ref, gout_ref, wq_ref, wk_ref, wv_ref, wo_ref, up_ref, down_ref, dq_ref, dv_ref, uq_ref, uv_ref) = refs[:12]
+        (x_hbm, gout_hbm, wq_ref, wk_ref, wv_ref, wo_ref, up_ref, down_ref, dq_ref, dv_ref, uq_ref, uv_ref) = refs[:12]
         (bq_ref, bv_ref, bup_ref) = refs[12:15]
         vector_refs, (seg_ref, live_ref) = refs[15:21], refs[21:23]
         (out_ref, gin_ref, glq_ref, glv_ref) = refs[23:27]
         (wq, wk, wv, wo, q, k, v, probs, ctx, n1, s1, act, slope, acc, mask, u_t) = refs[27:43]
         (a_ref, b_ref, c_ref, bias, biases, part, near, far) = refs[43:51]
-        (send, recv, bias_send, bias_recv, near_send, near_recv, far_send, far_recv) = refs[51:]
+        (send, recv, bias_send, bias_recv, near_send, near_recv, far_send, far_recv) = refs[51:59]
+        (x_ref, gout_ref, load) = refs[59:]
     else:
         (x_ref, gout_ref, a_ref, b_ref, c_ref, biases_ref, dq_ref, dv_ref) = refs[:8]
         vector_refs, (seg_ref, live_ref) = refs[8:14], refs[14:16]
@@ -285,10 +286,21 @@
         others_d = [lax.rem(me_d + i, dps) for i in range(1, dps)]
         seg_rows = pl.ds(pl.multiple_of(me_t * (rows // LANES), rows // LANES), rows // LANES)
         barrier = pltpu.get_barrier_semaphore()
-        for other in others_t:
-            pl.semaphore_signal(barrier, inc=1, device_id=(me_d, other), device_id_type=BY_MESH)
-        for other in others_d:
-            pl.semaphore_signal(barrier, inc=1, device_id=(other, me_t), device_id_type=BY_MESH)
+        neighbours = [(me_d, other) for other in others_t] + [gather.peer("y")]
+        for peer in neighbours:
+            pl.semaphore_signal(barrier, inc=1, device_id=peer, device_id_type=BY_MESH)
+        for kind in "+-":
+
+            @pl.when(gather.there_is(kind))
+            def _(kind=kind):
+                pl.semaphore_signal(barrier, inc=1, device_id=gather.peer(kind), device_id_type=BY_MESH)
+
+        loads = [
+            pltpu.make_async_copy(source, target, load.at[i])
+            for i, (source, target) in enumerate(((x_hbm, x_ref), (gout_hbm, gout_ref)))
+        ]
+        for copy in loads:
+            copy.start()
 
         mine = pl.ds(pl.multiple_of(me_d * depth, depth), depth)
         across = wq_ref.shape[1]
@@ -307,7 +319,8 @@
         bias[me_t, 0:1, :] = jnp.reshape(bup_ref[...], (1, width))
         bias[me_t, 1:2, 0:across] = jnp.reshape(bq_ref[...], (1, across)) * SCORE_SCALE
         bias[me_t, 1:2, 256 : 256 + across] = jnp.reshape(bv_ref[...], (1, across))
-        pl.semaphore_wait(barrier, len(others_t) + len(others_d))
+        outer = lax.rem(gather.z, 3) == 0
+        pl.semaphore_wait(barrier, len(neighbours) + jnp.where(outer, 1, 2))
 
         def bias_copy(i):
             return pltpu.make_async_remote_copy(
@@ -369,6 +382,8 @@
                 at = SPAN_STARTS[block] + j * LANES
                 mask[seq, at : at + LANES, :] = jnp.where(seen, 0.0, NEG_FILL)
 
+    if plan is not None:
+        loads[0].wait()
     adapters_down = jnp.concatenate([dq_ref[...].astype(WIDE), dv_ref[...].astype(WIDE)], axis=0)
     u_t[...] = mm_nt(adapters_down.astype(NARROW), x_ref[...]).astype(NARROW)
 
@@ -481,7 +496,7 @@
         out_ref[at, :] = (normed * gain1 + shift1).astype(NARROW)
         return carry
 
-    lax.fori_loop(0, rows // 256, first_norm, 0)
+    lax.fori_loop(0, rows // 256, first_norm, 0, unroll=2)
 
     def up(group, carry):
         ticks("up", group)
@@ -497,6 +512,8 @@
     ticks("before up")
     lax.fori_loop(0, groups, up, 0)
     ticks("before down")
+    if plan is not None:
+        loads[1].wait()
 
     def second_norm(step, carry):
         at = pl.ds(pl.multiple_of(step * 256, 256), 256)
@@ -511,7 +528,7 @@
         acc[at, :] = inverse * (e - row_mean(e) - normed * row_mean(e * normed))
         return carry
 
-    lax.fori_loop(0, rows // 256, second_norm, 0)
+    lax.fori_loop(0, rows // 256, second_norm, 0, unroll=2)
 
     def down_back(step, carry):
         at = pl.ds(pl.multiple_of(step * 256, 256), 256)
@@ -529,24 +546,25 @@
         ctx[at, :] = mm(first.astype(NARROW), wo[...]).astype(NARROW)
         return carry
 
-    lax.fori_loop(0, rows // 256, down_back, 0)
+    lax.fori_loop(0, rows // 256, down_back, 0, unroll=2)
 
     def attend_back(step, carry):
         items = work_of(step)
+        grads = [stacked(ctx[here, at]) for _, _, here, _, at, _, _ in items]
+        rows_q = [stacked(q[here, at]) for _, _, here, _, at, _, _ in items]
         grad_q, grad_k, grad_v = [], {}, {}
-        for index, seq, here, there, at, span, block in items:
-            grads = stacked(ctx[here, at])
+        for n, (index, seq, here, there, at, span, block) in enumerate(items):
             weights = probs[index, span, :]
-            part = weights.astype(WIDE) * mm_nt(v[there, at], grads)
+            part = weights.astype(WIDE) * mm_nt(v[there, at], grads[n])
             inside = jnp.sum(part, axis=0, keepdims=True)
             grad_scores = (part - weights.astype(WIDE) * inside).astype(NARROW)
+            for_keys = mm(grad_scores, rows_q[n])
+            for_values = mm(weights, grads[n])
             grad_q.append(merged(mm_tn(grad_scores, k[there, at])))
-            for_keys = mm(grad_scores, stacked(q[here, at]))
-            for_values = mm(weights, grads)
             start, stop = KEY_SPANS[block]
             for j in range((stop - start) // LANES):
                 rows_here = slice(j * LANES, (j + 1) * LANES)
-                key = (len(grad_q) - 1) // 4, start // LANES + j
+                key = n // 4, start // LANES + j
                 for grad, more in ((grad_k, for_keys), (grad_v, for_values)):
                     grad[key] = grad[key] + more[rows_here] if key in grad else more[rows_here]
         for (_, _, here, _, at, _, _), grad in zip(items, grad_q):
@@ -690,7 +708,8 @@
             pltpu.VMEM((ADAPTER_RANK, width // groups), WIDE),
             pltpu.VMEM((ADAPTER_RANK, width // groups), WIDE),
         ),
-        in_specs=[pl.BlockSpec(memory_space=pltpu.VMEM)] * len(operands),
+        in_specs=[pl.BlockSpec(memory_space=pl.ANY)] * 2
+        + [pl.BlockSpec(memory_space=pltpu.VMEM)] * (len(operands) - 2),
         out_specs=[pl.BlockSpec(memory_space=pltpu.VMEM)] * 4,
         scratch_shapes=scratch(rows, width, groups * width)
         + [
@@ -710,6 +729,9 @@
             signals((groups - 1,)),
             signals((dps - 1,)),
             signals((dps - 1,)),
+            pltpu.VMEM((rows, width), NARROW),
+            pltpu.VMEM((rows, width), NARROW),
+            signals((2,)),
         ],
         compiler_params=pltpu.CompilerParams(
             collective_id=0, has_side_effects=True, vmem_limit_bytes=59 << 20

time: 118 us -> 110 us (0.932)
  Pallas kernels: 114 us -> 106 us
    pallas_call x1, Pallas kernels: 114 us -> 106 us  [run_layer_and_gather(): pl.pallas_call(functools.partial(kernel, PLAN), out_shape=(pltpu.VMEM((ro...]
where the time goes in v6:
time: 110 us
  Pallas kernels  106 us (96%)
  local copies, waits for them, and re-layouts  3.48 us (3%)
    pallas_call x1, Pallas kernels, run_layer_and_gather(): pl.pallas_call(functools.partial(kernel, PLAN), out_shape=(pltpu.VMEM((ro...  106 us
    unnamed x4, local copies, waits for them, and re-layouts  3.48 us

profile of v6, /device:TPU:0, one launch (start us, length us, event | category | flops | bytes accessed | tf_op | source)
XLA Modules:
  0.0 110.0 jit_solution(8733947882361745975)
XLA Ops:
  0.6 105.9 %shard_map.246 = (bf16[1024,768]{1,0:T(8,128)(2,1)S(1)}, bf16[1024,768]{1,0:T(8,128)(2,1)S(1)}, f32[8,192]{1,0:T(8,128)S(1)}, f32[8,192]{1,0:T(8,128)S(1)}) custom-call(bf16[1024,768]{1,0:T(8,128)(2,1)} %refs_0_.1, bf16[1024,768]{1,0:T(8,128)(2,1)} %refs_1_.1, bf16[96,192]{1,0:T(8,128)(2,1)} %refs_2_.1, bf16[96,192]{1,0:T(8,128)(2,1)} %refs_3_.1, ...), custom_call_target="tpu_custom_call" | custom-call | tf_op jit(solution)/shard_map/pallas_call | solution.py:703
  106.5 1.1 %copy.31 = bf16[1024,768]{1,0:T(8,128)(2,1)} copy(bf16[1024,768]{1,0:T(8,128)(2,1)S(1)} %get-tuple-element.4) | data formatting | bytes 3145728
  107.7 0.6 copy.33
  108.3 0.6 copy.34
  108.9 1.1 %copy.32 = bf16[1024,768]{1,0:T(8,128)(2,1)} copy(bf16[1024,768]{1,0:T(8,128)(2,1)S(1)} %get-tuple-element.5) | data formatting | bytes 3145728

commit v7 on v6

--- a/solution.py
+++ b/solution.py
@@ -70,43 +70,46 @@
     },
     "start": {
         0: steps_of(
-            100, 101, 8, 4, 2, 200, 23, 5, 6, 102, 13, 28, 25, 204, 3, 29, 18, 14, 33, 10, 30,
-            108, 15, 19, 20, 123, 24, 7, 11, 9, 201, 113, 34, 35, 16, 17, 202,
+            100, 101, 23, 4, 200, 8, 5, 2, 13, 28, 202, 3, 25, 104,
         ),
     },
     "masked": {
         0: steps_of(
-            128, 26, 12, 21, 22, 36, 37, 27, 104, 31, 32, 206,
+            10, 29, 33, 201, 14, 30, 108, 18, 24, 6, 7, 9, 15, 26, 20, 35, 19, 123, 34, 106, 102,
+            223, 31, 11, 204, 12, 16, 208, 21, 27, 17, 22, 32, 36, 37, 113, 128, 105, 103,
         ) + [(0, name) for name in FROM_CORE],
     },
     "project": {
         0: steps_of(
-            208, 130, 133, 118, 223, 103,
+            228, 213,
         ),
         1: steps_of(
-            105,
-        ),
-        2: steps_of(
-            228, 114,
+            115, 130,
         ),
     },
     "attend": {
         0: steps_of(
-            213, 119, 129,
+            203, 133, 118,
         ),
         2: steps_of(
-            115, 230, 203, 205, 120, 134,
+            125, 129, 206, 107, 114, 110, 131,
         ),
         3: steps_of(
-            125, 109, 135, 110, 124,
+            124, 135, 116, 134, 120, 109, 205, 207, 119,
         ),
     },
     "first_norm": {
+        0: steps_of(
+            214, 230, 117, 215, 111, 132, 126,
+        ),
+        1: steps_of(
+            136,
+        ),
         2: steps_of(
-            126, 231, 116, 117, 121, 106, 107, 229, 218, 127,
+            233, 127, 121,
         ),
         3: steps_of(
-            122, 136, 137, 214, 111, 112, 233, 215, 131, 132,
+            229, 112, 137, 122, 218,
         ),
     },
     "before up": {
@@ -115,11 +118,17 @@
         ) + [(1, name) for name in FROM_CORE],
     },
     "up": {
+        0: steps_of(
+            209,
+        ),
         1: steps_of(
-            219, 235, 234, 207, 220, 225, 216, 209, 217, 210, 224, 232,
+            235, 220, 234, 224, 210, 225,
+        ),
+        2: steps_of(
+            219, 231, 216,
         ),
         3: steps_of(
-            221, 222, 211, 212, 226, 227, 236, 237,
+            221, 211, 236, 212, 217, 237, 222, 232, 226, 227,
         ),
     },
     "before down": {

time: 110 us -> 108 us (0.982)
  Pallas kernels: 106 us -> 104 us
    pallas_call x1, Pallas kernels: 106 us -> 104 us  [run_layer_and_gather(): pl.pallas_call(functools.partial(kernel, PLAN), out_shape=(pltpu.VMEM((ro...]
where the time goes in v7:
time: 108 us
  Pallas kernels  104 us (96%)
  local copies, waits for them, and re-layouts  3.48 us (3%)
    pallas_call x1, Pallas kernels, run_layer_and_gather(): pl.pallas_call(functools.partial(kernel, PLAN), out_shape=(pltpu.VMEM((ro...  104 us
    unnamed x4, local copies, waits for them, and re-layouts  3.48 us

profile of v7, /device:TPU:0, one launch (start us, length us, event | category | flops | bytes accessed | tf_op | source)
XLA Modules:
  0.0 108.3 jit_solution(15238226540136677090)
XLA Ops:
  0.6 104.2 %shard_map.246 = (bf16[1024,768]{1,0:T(8,128)(2,1)S(1)}, bf16[1024,768]{1,0:T(8,128)(2,1)S(1)}, f32[8,192]{1,0:T(8,128)S(1)}, f32[8,192]{1,0:T(8,128)S(1)}) custom-call(bf16[1024,768]{1,0:T(8,128)(2,1)} %refs_0_.1, bf16[1024,768]{1,0:T(8,128)(2,1)} %refs_1_.1, bf16[96,192]{1,0:T(8,128)(2,1)} %refs_2_.1, bf16[96,192]{1,0:T(8,128)(2,1)} %refs_3_.1, ...), custom_call_target="tpu_custom_call" | custom-call | tf_op jit(solution)/shard_map/pallas_call | solution.py:712
  104.8 1.1 %copy.31 = bf16[1024,768]{1,0:T(8,128)(2,1)} copy(bf16[1024,768]{1,0:T(8,128)(2,1)S(1)} %get-tuple-element.4) | data formatting | bytes 3145728
  106.0 0.6 copy.33
  106.6 0.6 copy.34
  107.2 1.1 %copy.32 = bf16[1024,768]{1,0:T(8,128)(2,1)} copy(bf16[1024,768]{1,0:T(8,128)(2,1)S(1)} %get-tuple-element.5) | data formatting | bytes 3145728

commit v8 on v7

--- a/solution.py
+++ b/solution.py
@@ -460,7 +460,7 @@
     def merged(tile):
         return jnp.where(lane < HEAD_DIM, tile[:LANES], tile[LANES:]).astype(NARROW)
 
-    def work_of(step):
+    def work_of(step, together=together):
         items = []
         for one in range(together):
             index = step * together + one
@@ -558,7 +558,7 @@
     lax.fori_loop(0, rows // 256, down_back, 0, unroll=2)
 
     def attend_back(step, carry):
-        items = work_of(step)
+        items = work_of(step, pairs)
         grads = [stacked(ctx[here, at]) for _, _, here, _, at, _, _ in items]
         rows_q = [stacked(q[here, at]) for _, _, here, _, at, _, _ in items]
         grad_q, grad_k, grad_v = [], {}, {}
@@ -584,7 +584,7 @@
             v[here, at] = grad_v[one, kb].astype(NARROW)
         return carry
 
-    lax.fori_loop(0, steps, attend_back, 0)
+    lax.fori_loop(0, seqs, attend_back, 0)
 
     grad_q = mm(u_t[0:8, :], q[...]) * (ADAPTER_SCALE * SCORE_SCALE)
     grad_v = mm(u_t[8:16, :], v[...]) * ADAPTER_SCALE

time: 108 us -> 107 us (level)
  no operation moved by 1% of the time
where the time goes in v8:
time: 107 us
  Pallas kernels  103 us (96%)
  local copies, waits for them, and re-layouts  3.48 us (3%)
    pallas_call x1, Pallas kernels, run_layer_and_gather(): pl.pallas_call(functools.partial(kernel, PLAN), out_shape=(pltpu.VMEM((ro...  103 us
    unnamed x4, local copies, waits for them, and re-layouts  3.48 us

profile of v8, /device:TPU:0, one launch (start us, length us, event | category | flops | bytes accessed | tf_op | source)
XLA Modules:
  0.0 107.2 jit_solution(11119541397993098360)
XLA Ops:
  0.6 103.1 %shard_map.246 = (bf16[1024,768]{1,0:T(8,128)(2,1)S(1)}, bf16[1024,768]{1,0:T(8,128)(2,1)S(1)}, f32[8,192]{1,0:T(8,128)S(1)}, f32[8,192]{1,0:T(8,128)S(1)}) custom-call(bf16[1024,768]{1,0:T(8,128)(2,1)} %refs_0_.1, bf16[1024,768]{1,0:T(8,128)(2,1)} %refs_1_.1, bf16[96,192]{1,0:T(8,128)(2,1)} %refs_2_.1, bf16[96,192]{1,0:T(8,128)(2,1)} %refs_3_.1, ...), custom_call_target="tpu_custom_call" | custom-call | tf_op jit(solution)/shard_map/pallas_call | solution.py:712
  103.8 1.1 %copy.31 = bf16[1024,768]{1,0:T(8,128)(2,1)} copy(bf16[1024,768]{1,0:T(8,128)(2,1)S(1)} %get-tuple-element.4) | data formatting | bytes 3145728
  104.9 0.6 copy.33
  105.5 0.6 copy.34
  106.1 1.1 %copy.32 = bf16[1024,768]{1,0:T(8,128)(2,1)} copy(bf16[1024,768]{1,0:T(8,128)(2,1)S(1)} %get-tuple-element.5) | data formatting | bytes 3145728

commit v9 on v8

--- a/solution.py
+++ b/solution.py
@@ -525,7 +525,7 @@
         loads[1].wait()
 
     def second_norm(step, carry):
-        at = pl.ds(pl.multiple_of(step * 256, 256), 256)
+        at = pl.ds(pl.multiple_of(step * 512, 512), 512)
         r = n1[at, :] * gain1 + shift1 + down_bias
         for group in range(groups):
             r = r + mm_nt(act[at, group * width : (group + 1) * width], c_ref[group])
@@ -537,10 +537,10 @@
         acc[at, :] = inverse * (e - row_mean(e) - normed * row_mean(e * normed))
         return carry
 
-    lax.fori_loop(0, rows // 256, second_norm, 0, unroll=2)
+    lax.fori_loop(0, rows // 512, second_norm, 0)
 
     def down_back(step, carry):
-        at = pl.ds(pl.multiple_of(step * 256, 256), 256)
+        at = pl.ds(pl.multiple_of(step * 512, 512), 512)
         second = acc[at, :]
         low = second.astype(NARROW)
         total = second
@@ -555,7 +555,7 @@
         ctx[at, :] = mm(first.astype(NARROW), wo[...]).astype(NARROW)
         return carry
 
-    lax.fori_loop(0, rows // 256, down_back, 0, unroll=2)
+    lax.fori_loop(0, rows // 512, down_back, 0)
 
     def attend_back(step, carry):
         items = work_of(step, pairs)

time: 107 us -> 107 us (level)
  no operation moved by 1% of the time
where the time goes in v9:
time: 107 us
  Pallas kernels  103 us (96%)
  local copies, waits for them, and re-layouts  3.48 us (3%)
    pallas_call x1, Pallas kernels, run_layer_and_gather(): pl.pallas_call(functools.partial(kernel, PLAN), out_shape=(pltpu.VMEM((ro...  103 us
    unnamed x4, local copies, waits for them, and re-layouts  3.48 us

profile of v9, /device:TPU:0, one launch (start us, length us, event | category | flops | bytes accessed | tf_op | source)
XLA Modules:
  0.0 106.9 jit_solution(10664580387286678581)
XLA Ops:
  0.6 102.8 %shard_map.246 = (bf16[1024,768]{1,0:T(8,128)(2,1)S(1)}, bf16[1024,768]{1,0:T(8,128)(2,1)S(1)}, f32[8,192]{1,0:T(8,128)S(1)}, f32[8,192]{1,0:T(8,128)S(1)}) custom-call(bf16[1024,768]{1,0:T(8,128)(2,1)} %refs_0_.1, bf16[1024,768]{1,0:T(8,128)(2,1)} %refs_1_.1, bf16[96,192]{1,0:T(8,128)(2,1)} %refs_2_.1, bf16[96,192]{1,0:T(8,128)(2,1)} %refs_3_.1, ...), custom_call_target="tpu_custom_call" | custom-call | tf_op jit(solution)/shard_map/pallas_call | solution.py:712
  103.4 1.1 %copy.31 = bf16[1024,768]{1,0:T(8,128)(2,1)} copy(bf16[1024,768]{1,0:T(8,128)(2,1)S(1)} %get-tuple-element.4) | data formatting | bytes 3145728
  104.6 0.6 copy.33
  105.2 0.6 copy.34
  105.8 1.1 %copy.32 = bf16[1024,768]{1,0:T(8,128)(2,1)} copy(bf16[1024,768]{1,0:T(8,128)(2,1)S(1)} %get-tuple-element.5) | data formatting | bytes 3145728
